TPU v7x, 32 devices: a whole 2x2x4 slice. The times are simulated.
32 devices in a mesh: rows: 8 (over z, x), heads: 4 (over y, core).
Axes of the slice: x: 2, y: 2, z: 4, core: 2. Of those that a mesh axis runs over, the one named last changes fastest.
Arguments:
- pixels: bfloat16 [8192, 1024], P('rows'), may hold values from -6 to 6
- crop_ids: int32 [8192], P('rows'), may hold values from 0 to 3, never falling along the last dimension, each value on 1 to 4096 neighbouring positions
- first_gain: float32 [1024], replicated, may hold values from 0.1 to 1.9
- query_weight: bfloat16 [1024, 1024], P(None, 'heads'), may hold values from -0.1875 to 0.1875
- key_weight: bfloat16 [1024, 1024], P(None, 'heads'), may hold values from -0.1875 to 0.1875
- value_weight: bfloat16 [1024, 1024], P(None, 'heads'), may hold values from -0.1875 to 0.1875
- out_weight: bfloat16 [1024, 1024], P('heads'), may hold values from -0.75 to 0.75
- second_gain: float32 [1024], replicated, may hold values from 0.1 to 1.9
- up_weight: bfloat16 [1024, 4096], P(None, 'heads'), may hold values from -0.1875 to 0.1875
- down_weight: bfloat16 [4096, 1024], P('heads'), may hold values from -0.09375 to 0.09375
- cotangent: bfloat16 [8192, 1024], P('rows'), may hold values from -6 to 6
Outputs:
- result: bfloat16 [8192, 1024], P('rows')
- pixel_gradient: float32 [8192, 1024], P('rows')
- first_gain_gradient: float32 [1024], P('rows')
- query_gradient: float32 [1024, 1024], P('rows', 'heads')
- key_gradient: float32 [1024, 1024], P('rows', 'heads')
- value_gradient: float32 [1024, 1024], P('rows', 'heads')
- out_gradient: float32 [1024, 1024], P('heads', 'rows')
- second_gain_gradient: float32 [1024], P('rows')
- up_gradient: float32 [1024, 4096], P('rows', 'heads')
- down_gradient: float32 [4096, 1024], P('heads', 'rows')
Inputs may be any that keep to these rules, and one draw needn't show every extreme that they name: `crop_ids`: crop ids never fall along the tokens; each crop holds 1 to 4096 consecutive tokens, and one holds exactly 4096.
All inputs are finite; a program needn't handle non-finite values.
Results may differ from a plain program's by a relative error of at most 0.017.
Values sent between devices are 32-bit elements; how exact they have to be, the bound alone decides.
A program may use at most 128 MiB of HBM per device.

v0:
```python
import jax
import jax.numpy as jnp
from jax import lax
from jax.sharding import PartitionSpec as P

HEAD = 64


EPSILON = 1e-05
PRECISE = lax.Precision.HIGHEST


def carried_in(part, axis, combine, identity, reverse):
    count = lax.axis_size(axis)
    place = lax.axis_index(axis)
    ahead = count - 1 - place if reverse else place
    gathered = jax.tree.map(lambda a: lax.all_gather(a, axis), part)
    state = jax.tree.map(lambda a, e: jnp.zeros_like(a) + jnp.asarray(e, a.dtype), part, identity)

    def one(hop, state):
        source = count - 1 - hop if reverse else hop
        return combine(
            state, jax.tree.map(lambda a: lax.dynamic_index_in_dim(a, source, 0, False), gathered)
        )

    return lax.fori_loop(0, ahead, one, state)


def layer_norm(value, gain):
    middle = jnp.mean(value, axis=-1, keepdims=True)
    centred = value - middle
    spread = jnp.mean(centred * centred, axis=-1, keepdims=True)
    return centred * lax.rsqrt(spread + EPSILON) * gain


def feature(value):
    return jax.nn.elu(value) + 1.0


def matmul(left, right):
    return jnp.dot(left, right, preferred_element_type=jnp.float32)


def inner_left(left, right):
    return lax.dot_general(
        left, right, (((0,), (0,)), ((), ())), preferred_element_type=jnp.float32
    )


def inner_right(left, right):
    return lax.dot_general(
        left, right, (((1,), (1,)), ((), ())), preferred_element_type=jnp.float32
    )


def join_states(earlier, later):
    vacant = later[2] < 0
    same_crop = (earlier[2] == later[2]).astype(jnp.float32)
    return (
        jnp.where(vacant, earlier[0], later[0] + same_crop * earlier[0]),
        jnp.where(vacant, earlier[1], later[1] + same_crop * earlier[1]),
        jnp.where(vacant, earlier[2], later[2]),
    )


def on_device(
    pixels,
    crop_ids,
    first_gain,
    query_weight,
    key_weight,
    value_weight,
    out_weight,
    second_gain,
    up_weight,
    down_weight,
    cotangent,
):
    tokens = pixels.astype(jnp.float32)
    labels = crop_ids.astype(jnp.float32)
    length = tokens.shape[0]
    heads_here = query_weight.shape[1] // HEAD
    blocked = (length, heads_here, HEAD)
    normed = layer_norm(tokens, first_gain)
    normed_low = normed.astype(jnp.bfloat16)
    query = matmul(normed_low, query_weight)
    key_raw = matmul(normed_low, key_weight)
    values = matmul(normed_low, value_weight).astype(jnp.bfloat16).reshape(blocked)
    query_feature = feature(query).astype(jnp.bfloat16).reshape(blocked)
    key_feature = feature(key_raw).astype(jnp.bfloat16).reshape(blocked)
    places = jnp.arange(length)
    allowed = (places[:, None] >= places[None, :]) & (crop_ids[:, None] == crop_ids[None, :])
    scores = jnp.einsum(
        "ihe,jhe->hij", query_feature, key_feature, preferred_element_type=jnp.float32
    )
    scores = jnp.where(allowed[None], scores, 0.0)
    scores_low = scores.astype(jnp.bfloat16)
    inner_total = jnp.sum(scores, axis=2).T
    tail_mask = crop_ids == crop_ids[length - 1]
    block_state = jnp.einsum(
        "ihe,ihf->hef",
        jnp.where(tail_mask[:, None, None], key_feature, 0),
        values,
        preferred_element_type=jnp.float32,
    )
    block_total = jnp.einsum(
        "ihe,i->he", key_feature, tail_mask.astype(jnp.bfloat16), preferred_element_type=jnp.float32
    )
    start = (jnp.zeros_like(block_state), jnp.zeros_like(block_total), jnp.float32(-1.0))
    prefix_state, prefix_total, latest = carried_in(
        (block_state, block_total, labels[length - 1]), "rows", join_states, start, False
    )
    matching = (labels == latest).astype(jnp.float32)
    prefix_low = prefix_state.astype(jnp.bfloat16)
    query_wide = query_feature.astype(jnp.float32)
    numerator = jnp.einsum("hij,jhe->ihe", scores_low, values, preferred_element_type=jnp.float32)
    numerator = numerator + matching[:, None, None] * jnp.einsum(
        "ihe,hef->ihf", query_feature, prefix_low, preferred_element_type=jnp.float32
    )
    denominator = inner_total + matching[:, None] * jnp.einsum(
        "ihe,he->ih", query_wide, prefix_total, precision=PRECISE
    )
    attended = numerator / denominator[:, :, None]
    attended_low = attended.reshape(length, -1).astype(jnp.bfloat16)
    hidden = tokens + lax.psum(matmul(attended_low, out_weight), "heads")
    normed_again = layer_norm(hidden, second_gain)
    normed_again_low = normed_again.astype(jnp.bfloat16)
    upward = matmul(normed_again_low, up_weight)
    middle = jax.nn.gelu(upward).astype(jnp.bfloat16)
    result = hidden + lax.psum(matmul(middle, down_weight), "heads")
    down_gradient = inner_left(middle, cotangent)
    middle_back = inner_right(cotangent, down_weight)
    unused, gelu_back = jax.vjp(jax.nn.gelu, upward)
    upward_low = gelu_back(middle_back)[0].astype(jnp.bfloat16)
    up_gradient = inner_left(normed_again_low, upward_low)
    normed_again_back = lax.psum(inner_right(upward_low, up_weight), "heads")
    unused, second_back = jax.vjp(layer_norm, hidden, second_gain)
    hidden_part, second_gain_gradient = second_back(normed_again_back)
    hidden_gradient = cotangent.astype(jnp.float32) + hidden_part
    hidden_low = hidden_gradient.astype(jnp.bfloat16)
    out_gradient = inner_left(attended_low, hidden_low)
    attended_back = inner_right(hidden_low, out_weight).reshape(blocked)
    numerator_low = (attended_back / denominator[:, :, None]).astype(jnp.bfloat16)
    denominator_back = -jnp.sum(attended_back * attended, axis=2) / denominator
    scores_back = (
        jnp.einsum("ihe,jhe->hij", numerator_low, values, preferred_element_type=jnp.float32)
        + denominator_back.T[:, :, None]
    )
    scores_back = jnp.where(allowed[None], scores_back, 0.0).astype(jnp.bfloat16)
    value_back = jnp.einsum(
        "hij,ihe->jhe", scores_low, numerator_low, preferred_element_type=jnp.float32
    )
    query_feature_back = jnp.einsum(
        "hij,jhe->ihe", scores_back, key_feature, preferred_element_type=jnp.float32
    )
    query_feature_back = query_feature_back + matching[:, None, None] * (
        jnp.einsum("ihf,hef->ihe", numerator_low, prefix_low, preferred_element_type=jnp.float32)
        + denominator_back[:, :, None] * prefix_total[None]
    )
    key_feature_back = jnp.einsum(
        "hij,ihe->jhe", scores_back, query_feature, preferred_element_type=jnp.float32
    )
    head_mask = crop_ids == crop_ids[0]
    head_query = jnp.where(head_mask[:, None, None], query_feature, 0)
    back_state = jnp.einsum(
        "ihe,ihf->hef", head_query, numerator_low, preferred_element_type=jnp.float32
    )
    back_total = jnp.einsum(
        "ihe,ih->he", head_query.astype(jnp.float32), denominator_back, precision=PRECISE
    )
    suffix_state, suffix_total, following = carried_in(
        (back_state, back_total, labels[0]), "rows", join_states, start, True
    )
    later_mask = (labels == following).astype(jnp.float32)
    suffix_low = suffix_state.astype(jnp.bfloat16)
    key_feature_back = key_feature_back + later_mask[:, None, None] * (
        jnp.einsum("jhf,hef->jhe", values, suffix_low, preferred_element_type=jnp.float32)
        + suffix_total[None]
    )
    value_back = value_back + later_mask[:, None, None] * jnp.einsum(
        "jhe,hef->jhf", key_feature, suffix_low, preferred_element_type=jnp.float32
    )
    value_low = value_back.reshape(length, -1).astype(jnp.bfloat16)
    unused, query_back = jax.vjp(feature, query)
    query_low = query_back(query_feature_back.reshape(length, -1))[0].astype(jnp.bfloat16)
    unused, key_back = jax.vjp(feature, key_raw)
    key_low = key_back(key_feature_back.reshape(length, -1))[0].astype(jnp.bfloat16)
    query_gradient = inner_left(normed_low, query_low)
    key_gradient = inner_left(normed_low, key_low)
    value_gradient = inner_left(normed_low, value_low)
    normed_terms = (
        inner_right(query_low, query_weight)
        + inner_right(key_low, key_weight)
        + inner_right(value_low, value_weight)
    )
    normed_back = lax.psum(normed_terms, "heads")
    unused, first_back = jax.vjp(layer_norm, tokens, first_gain)
    pixel_part, first_gain_gradient = first_back(normed_back)
    pixel_gradient = hidden_gradient + pixel_part
    (
        query_gradient,
        key_gradient,
        value_gradient,
        out_gradient,
        up_gradient,
        down_gradient,
        first_gain_gradient,
        second_gain_gradient,
    ) = (
        lax.psum_scatter(query_gradient, "rows", scatter_dimension=0, tiled=True),
        lax.psum_scatter(key_gradient, "rows", scatter_dimension=0, tiled=True),
        lax.psum_scatter(value_gradient, "rows", scatter_dimension=0, tiled=True),
        lax.psum_scatter(out_gradient, "rows", scatter_dimension=1, tiled=True),
        lax.psum_scatter(up_gradient, "rows", scatter_dimension=0, tiled=True),
        lax.psum_scatter(down_gradient, "rows", scatter_dimension=1, tiled=True),
        lax.psum_scatter(first_gain_gradient, "rows", scatter_dimension=0, tiled=True),
        lax.psum_scatter(second_gain_gradient, "rows", scatter_dimension=0, tiled=True),
    )
    return (
        result.astype(jnp.bfloat16),
        pixel_gradient,
        first_gain_gradient,
        query_gradient,
        key_gradient,
        value_gradient,
        out_gradient,
        second_gain_gradient,
        up_gradient,
        down_gradient,
    )


def solution(mesh):
    return jax.shard_map(
        on_device,
        mesh=mesh,
        in_specs=(
            P("rows", None),
            P("rows"),
            P(),
            P(None, "heads"),
            P(None, "heads"),
            P(None, "heads"),
            P("heads", None),
            P(),
            P(None, "heads"),
            P("heads", None),
            P("rows", None),
        ),
        out_specs=(
            P("rows", None),
            P("rows", None),
            P("rows"),
            P("rows", "heads"),
            P("rows", "heads"),
            P("rows", "heads"),
            P("heads", "rows"),
            P("rows"),
            P("rows", "heads"),
            P("heads", "rows"),
        ),
        check_vma=False,
    )
```

profile of v0, /device:TPU:0, one launch (start us, length us, event | category | flops | bytes accessed | tf_op | source)
XLA Modules:
  0.0 1065.2 jit_solution(8786772171648247113)
XLA Ops:
  7.3 1.4 fusion.75
  9.4 2.3 fusion.21
  11.7 1.3 broadcast_compare_fusion.1
  13.0 1.4 fusion.76
  16.0 2.0 convert_reduce_fusion
  18.0 2.3 fusion.19
  21.9 2.0 fusion.39
  24.2 27.8 %all-gather.4 = f32[8,4,64]{2,1,0:T(4,128)S(1)} all-gather(f32[1,4,64]{2,1,0:T(4,128)S(1)} %bitcast.185), channel_id=3, replica_groups=mesh['rows'=8,'heads'=4] {'rows'}, dimensions={0}, use_global_device_ids=true | all-gather | bytes 9216 | tf_op jit(solution)/shard_map/all_gather | solution.py:17
  52.3 34.7 %all-gather = f32[32,64,64]{2,1,0:T(8,128)} all-gather(f32[4,64,64]{2,1,0:T(8,128)S(1)} %fusion.46), channel_id=2, replica_groups=mesh['rows'=8,'heads'=4] {'rows'}, dimensions={0}, use_global_device_ids=true | all-gather | bytes 589824 | tf_op jit(solution)/shard_map/all_gather | solution.py:17
  87.0 19.9 %all-reduce.5 = (f32[8]{0:T(128)S(1)}, f32[8]{0:T(128)S(1)}) all-reduce(f32[8]{0:T(128)S(1)} %slice_dynamic-update-slice_fusion.1, f32[8]{0:T(128)S(1)} %slice_dynamic-update-slice_fusion), channel_id=1, replica_groups=mesh['rows'=8,'heads'=4] {'rows'}, use_global_device_ids=true, to_apply=%add | all-reduce | flops 16 | bytes 128
  107.0 3.6 fusion.45
  110.9 3.1 select_reduce_fusion
  114.1 2.0 fusion.23
  116.1 1.2 copy-done.40
  118.1 1.4 fusion.77
  120.2 2.8 fusion.80
  123.3 6.5 fusion.81
  129.8 100.1 %all-reduce.11.cloned.1.call-done = f32[1024,1024]{1,0:T(8,128)} async-done(((f32[1024,1024]{1,0:T(8,128)}), f32[1024,1024]{1,0:T(8,128)}) %all-reduce.11.cloned.1.call-update) | async-done | bytes 4194320 | tf_op jit(solution)/shard_map/psum | solution.py:125
  229.9 3.3 fusion.74
  234.0 3.0 copy-done.41
  237.0 6.7 fusion.18
  243.7 1.3 copy-done.42
  245.0 4.4 fusion.82
  249.8 1.1 copy-done.39
  251.0 6.8 fusion.69
  257.7 77.4 %all-reduce.13.cloned.1.call-done = f32[1024,1024]{1,0:T(8,128)} async-done(((f32[1024,1024]{1,0:T(8,128)}), f32[1024,1024]{1,0:T(8,128)}) %all-reduce.13.cloned.1.call-update) | async-done | bytes 4194320 | tf_op jit(solution)/shard_map/psum | solution.py:136
  335.2 4.5 multiply_reduce_fusion
  339.8 1.3 copy-done.14
  341.1 1.8 fusion.73
  343.5 1.5 copy-done.9
  346.4 1.3 slice-done
  348.0 1.3 slice-done.1
  349.2 3.7 fusion.22
  354.1 26.1 %all-gather.5 = f32[8,4,64]{2,1,0:T(4,128)S(1)} all-gather(f32[1,4,64]{2,1,0:T(4,128)S(1)} %bitcast.186), channel_id=5, replica_groups=mesh['rows'=8,'heads'=4] {'rows'}, dimensions={0}, use_global_device_ids=true | all-gather | bytes 9216 | tf_op jit(solution)/shard_map/all_gather | solution.py:17
  380.2 34.7 %all-gather.2 = f32[32,64,64]{2,1,0:T(8,128)} all-gather(f32[4,64,64]{2,1,0:T(8,128)S(1)} %fusion.50), channel_id=4, replica_groups=mesh['rows'=8,'heads'=4] {'rows'}, dimensions={0}, use_global_device_ids=true | all-gather | bytes 589824 | tf_op jit(solution)/shard_map/all_gather | solution.py:17
  414.9 25.0 %while.31 = (s32[]{:T(128)}, f32[4,64,64]{2,1,0:T(8,128)S(1)}, f32[4,64]{1,0:T(4,128)S(1)}, f32[]{:T(128)}, s32[]{:T(128)}, /*index=5*/f32[8]{0:T(128)S(1)}, f32...) while((s32[]{:T(128)}, f32[4,64,64]{2,1,0:T(8,128)S(1)}, ...), condition=%wide.region_14.15_spmd, body=%wide.region_13.14_spmd.sunk | while | flops 49930 | bytes 199933 | solution.py:26
  417.5 1.0 fusion.147
  421.0 1.0 fusion.147
  439.9 1.6 fusion.33
  441.5 1.5 fusion.29
  443.0 4.4 select_convert_fusion
  447.4 2.7 convolution_add_fusion
  450.1 1.6 fusion.25
  454.1 2.8 add_add_fusion.3
  457.0 3.7 fusion.88
  460.7 2.8 fusion.87
  463.6 1.8 fusion.85
  465.4 1.8 fusion.86
  467.5 7.5 fusion.71
  475.1 1.5 copy-done.16
  476.6 6.9 fusion.68
  484.3 122.4 %all-reduce.15.cloned.1.call-done = (f32[1024,1024]{1,0:T(8,128)}, f32[1024,1024]{1,0:T(8,128)}) async-done(((f32[1024,1024]{1,0:T(8,128)}, f32[1024,1024]{1,0:T(8,128)}), (f32[1024,1024]{1,0:T(8,128)}, f32[1024,1024]{1,0:T(8,128)})) %all-reduce.15.cloned.1.call-update) | async-done | bytes 8388624 | tf_op jit(solution)/shard_map/psum | solution.py:130
  606.8 3.2 fusion.20
  610.2 2.3 fusion.11
  612.5 21.9 %all-reduce.4 = (f32[1024]{0:T(1024)S(1)}, f32[1024]{0:T(1024)S(1)}) all-reduce(f32[1024]{0:T(1024)S(1)} %get-tuple-element.169, f32[1024]{0:T(1024)S(1)} %get-tuple-element.167), channel_id=6, replica_groups=mesh['rows'=8,'heads'=4] {'rows'}, use_global_device_ids=true, to_apply=%region_19.20.clone | all-reduce | flops 2048 | bytes 16384
  635.6 5.7 add_convert_fusion
  641.3 1.6 copy-done.12
  643.0 4.6 add_add_fusion.2
  647.6 27.2 %reduce-scatter.13.cloned.1.call-done = f32[256,128]{1,0:T(8,128)} async-done(((f32[256,1024]{1,0:T(8,128)}), f32[256,128]{1,0:T(8,128)}) %reduce-scatter.13.cloned.1.call-update) | async-done | bytes 131088 | tf_op jit(solution)/shard_map/reduce_scatter | solution.py:213
  674.8 66.7 %reduce-scatter.11.cloned.1.call-done = f32[128,256]{1,0:T(8,128)} async-done(((f32[1024,256]{1,0:T(8,128)}), f32[128,256]{1,0:T(8,128)}) %reduce-scatter.11.cloned.1.call-update) | async-done | bytes 131088 | tf_op jit(solution)/shard_map/reduce_scatter | solution.py:212
  741.5 66.4 %reduce-scatter.7.cloned.1.call-done = f32[128,256]{1,0:T(8,128)} async-done(((f32[1024,256]{1,0:T(8,128)}), f32[128,256]{1,0:T(8,128)}) %reduce-scatter.7.cloned.1.call-update) | async-done | bytes 131088 | tf_op jit(solution)/shard_map/reduce_scatter | solution.py:210
  807.9 66.7 %reduce-scatter.9.cloned.1.call-done = f32[128,256]{1,0:T(8,128)} async-done(((f32[1024,256]{1,0:T(8,128)}), f32[128,256]{1,0:T(8,128)}) %reduce-scatter.9.cloned.1.call-update) | async-done | bytes 131088 | tf_op jit(solution)/shard_map/reduce_scatter | solution.py:211
  874.6 91.1 %reduce-scatter.15.cloned.1.call-done = f32[128,1024]{1,0:T(8,128)} async-done(((f32[1024,1024]{1,0:T(8,128)}), f32[128,1024]{1,0:T(8,128)}) %reduce-scatter.15.cloned.1.call-update) | async-done | bytes 524304 | tf_op jit(solution)/shard_map/reduce_scatter | solution.py:214
  965.7 92.8 %reduce-scatter.17.cloned.1.call-done = f32[1024,128]{1,0:T(8,128)} async-done(((f32[1024,1024]{1,0:T(8,128)}), f32[1024,128]{1,0:T(8,128)}) %reduce-scatter.17.cloned.1.call-update) | async-done | bytes 524304 | tf_op jit(solution)/shard_map/reduce_scatter | solution.py:215
  (160 shorter events, 24.5 us)
Async XLA Ops:
  7.2 226.7 %copy-start = (bf16[1024,1024]{1,0:T(8,128)(2,1)S(1)}, bf16[1024,1024]{1,0:T(8,128)(2,1)}, u32[]{:S(2)}) copy-start(bf16[1024,1024]{1,0:T(8,128)(2,1)} %param.23) | copy-start | bytes 6291460
  7.2 13.2 %copy-start.37 = (f32[1024]{0:T(1024)S(1)}, f32[1024]{0:T(1024)}, u32[]{:S(2)}) copy-start(f32[1024]{0:T(1024)} %param.17) | copy-start | bytes 12292
  7.2 222.7 %all-reduce.11.cloned.1.call-start = ((), (), s32[]{:S(2)}) async-start(), calls=%async_computation.6 | async-start | bytes 8388608 | tf_op jit(solution)/shard_map/psum | solution.py:125
  13.0 7.3 copy-start.4
  16.0 5.0 copy-start.34
  20.3 1.5 copy-start.30
  21.1 3.1 copy-start.7
  21.9 30.1 %copy-start.32 = (bf16[1024,256]{0,1:T(8,128)(2,1)}, bf16[1024,256]{0,1:T(8,128)(2,1)S(1)}, u32[]{:S(2)}) copy-start(bf16[1024,256]{0,1:T(8,128)(2,1)S(1)} %convolution_convert_fusion) | copy-start | bytes 1572868
  21.9 85.1 %copy-start.28 = (bf16[1024,256]{1,0:T(8,128)(2,1)S(1)}, bf16[1024,256]{1,0:T(8,128)(2,1)}, u32[]{:S(2)}) copy-start(bf16[1024,256]{1,0:T(8,128)(2,1)} %param.18) | copy-start | bytes 1572868
  107.0 4.0 copy-start.24
  110.6 7.4 copy-start.21
  110.9 3.1 copy-start.33
  114.1 3.2 copy-start.40
  114.1 3.2 copy-start.36
  117.3 2.9 copy-start.20
  119.4 0.8 copy-start.18
  123.0 212.2 %all-reduce.13.cloned.1.call-start = ((), (), s32[]{:S(2)}) async-start(), calls=%async_computation.7 | async-start | bytes 8388608 | tf_op jit(solution)/shard_map/psum | solution.py:136
  233.2 10.5 copy-start.2
  233.2 0.7 copy-start.38
  233.2 3.7 copy-start.41
  243.7 1.3 copy-start.42
  249.4 1.6 copy-start.39
  249.4 357.4 %all-reduce.15.cloned.1.call-start = ((), (), s32[]{:S(2)}) async-start(), calls=%async_computation.14 | async-start | bytes 16777216 | tf_op jit(solution)/shard_map/psum | solution.py:130
  335.2 4.7 copy-start.3
  335.2 5.9 copy-start.14
  341.1 1.8 copy-start.15
  342.9 2.1 copy-start.9
  342.9 2.1 copy-start.19
  342.9 4.8 slice-start
  345.0 1.4 copy-start.13
  345.0 2.9 copy-start.25
  345.0 4.2 slice-start.1
  349.2 3.8 copy-start.22
  441.5 12.6 %copy-start.17 = (bf16[4,64,1024]{2,1,0:T(8,128)(2,1)}, bf16[4,64,1024]{2,1,0:T(8,128)(2,1)S(1)}, u32[]{:S(2)}) copy-start(bf16[4,64,1024]{2,1,0:T(8,128)(2,1)S(1)} %fusion.33) | copy-start | bytes 1572868
  443.0 4.4 copy-start.23
  450.1 1.7 copy-start.27
  450.1 2.0 copy-start.29
  451.7 1.2 copy-start.26
  452.1 1.2 copy-start.31
  452.9 1.2 copy-start.35
  456.9 3.8 copy-start.8
  457.0 217.8 %reduce-scatter.13.cloned.1.call-start = ((), (), s32[]{:S(2)}) async-start(), calls=%async_computation.11 | async-start | bytes 1179648 | tf_op jit(solution)/shard_map/reduce_scatter | solution.py:213
  460.7 280.8 %reduce-scatter.11.cloned.1.call-start = ((), (), s32[]{:S(2)}) async-start(), calls=%async_computation.10 | async-start | bytes 1179648 | tf_op jit(solution)/shard_map/reduce_scatter | solution.py:212
  463.6 344.3 %reduce-scatter.7.cloned.1.call-start = ((), (), s32[]{:S(2)}) async-start(), calls=%async_computation.8 | async-start | bytes 1179648 | tf_op jit(solution)/shard_map/reduce_scatter | solution.py:210
  465.4 409.2 %reduce-scatter.9.cloned.1.call-start = ((), (), s32[]{:S(2)}) async-start(), calls=%async_computation.9 | async-start | bytes 1179648 | tf_op jit(solution)/shard_map/reduce_scatter | solution.py:211
  467.2 498.5 %reduce-scatter.15.cloned.1.call-start = ((), (), s32[]{:S(2)}) async-start(), calls=%async_computation.12 | async-start | bytes 4718592 | tf_op jit(solution)/shard_map/reduce_scatter | solution.py:214
  475.0 1.6 copy-start.16
  475.1 583.4 %reduce-scatter.17.cloned.1.call-start = ((), (), s32[]{:S(2)}) async-start(), calls=%async_computation.13 | async-start | bytes 4718592 | tf_op jit(solution)/shard_map/reduce_scatter | solution.py:215
  483.5 123.2 %copy-start.5 = (bf16[1024,1024]{1,0:T(8,128)(2,1)S(1)}, bf16[1024,1024]{1,0:T(8,128)(2,1)}, u32[]{:S(2)}) copy-start(bf16[1024,1024]{1,0:T(8,128)(2,1)} %param.15) | copy-start | bytes 6291460
  606.8 3.4 copy-start.11
  635.6 5.7 copy-start.6
  635.6 5.7 copy-start.10
  635.6 7.4 copy-start.12
  643.0 415.5 %copy-start.1 = (bf16[1024,1024]{1,0:T(8,128)(2,1)S(1)}, bf16[1024,1024]{1,0:T(8,128)(2,1)}, u32[]{:S(2)}) copy-start(bf16[1024,1024]{1,0:T(8,128)(2,1)} %param.23) | copy-start | bytes 6291460
Sparse Core Ops, SparseCore 0:
  123.1 106.7 all-reduce.10
  249.5 85.5 all-reduce.12
  457.1 149.6 all-reduce.14
  610.6 64.1 reduce-scatter.12
  679.0 62.4 reduce-scatter.10
  745.3 62.5 reduce-scatter.6
  812.2 62.3 reduce-scatter.8
  878.8 86.8 reduce-scatter.14
  970.4 88.0 reduce-scatter.16
where the time goes:
time: 1070 us
  waiting for transfers between devices  711 us (66%)
  blocking collectives  165 us (15%)
  matrix products  87.1 us (8%)
  other arithmetic  44.3 us (4%)
  local copies, waits for them, and re-layouts  27.1 us (3%)
  between operations  15.5 us (1%)
  loops' own time  14 us (1%)
    all_gather x4, blocking collectives, carried_in(): gathered = jax.tree.map(lambda a: lax.all_gather(a, axis), part)  123 us
    psum x1, waiting for transfers between devices, on_device(): result = hidden + lax.psum(matmul(middle, down_weight), 'heads')  122 us
    psum x1, waiting for transfers between devices, on_device(): hidden = tokens + lax.psum(matmul(attended_low, out_weight), 'heads')  100 us
    reduce_scatter x1, waiting for transfers between devices, on_device(): lax.psum_scatter(down_gradient, 'rows', scatter_dimension=1, tiled=True)  92.8 us
    reduce_scatter x1, waiting for transfers between devices, on_device(): lax.psum_scatter(up_gradient, 'rows', scatter_dimension=0, tiled=True)  91.1 us
    psum x1, waiting for transfers between devices, on_device(): normed_again_back = lax.psum(inner_right(upward_low, up_weight), 'heads')  77.4 us
    reduce_scatter x1, waiting for transfers between devices, on_device(): lax.psum_scatter(key_gradient, 'rows', scatter_dimension=0, tiled=True)  66.7 us
    reduce_scatter x1, waiting for transfers between devices, on_device(): lax.psum_scatter(value_gradient, 'rows', scatter_dimension=0, tiled=True)  66.7 us
  transfers between devices with their start and end apart: 9, of which 9 were waited for; matrix products, arithmetic and copies ran while one was open for 5% of the time, Pallas kernels for 0%

commit v1 on v0

v1 whole, which is shorter than its diff:
```python
import functools
import math

import jax
import jax.numpy as jnp
from jax import lax
from jax.experimental import pallas as pl
from jax.experimental.pallas import tpu as pltpu
from jax.sharding import PartitionSpec as P

HEAD = 64
EPSILON = 1e-05
MESH = pl.DeviceIdType.MESH
LOW = jnp.bfloat16
WIDE = jnp.float32
LANES = 128
TILE = 256


def dot(left, right):
    return jnp.dot(left, right, preferred_element_type=WIDE)


def dot_left(left, right):
    return lax.dot_general(left, right, (((0,), (0,)), ((), ())), preferred_element_type=WIDE)


def dot_right(left, right):
    return lax.dot_general(left, right, (((1,), (1,)), ((), ())), preferred_element_type=WIDE)


def normalise(value):
    middle = jnp.mean(value, axis=-1, keepdims=True)
    centred = value - middle
    spread = jnp.mean(centred * centred, axis=-1, keepdims=True)
    scale = lax.rsqrt(spread + EPSILON)
    return centred * scale, scale


def normalise_back(unit, scale, gain, grad):
    scaled = grad * gain
    along = jnp.mean(scaled * unit, axis=-1, keepdims=True)
    return scale * (scaled - jnp.mean(scaled, axis=-1, keepdims=True) - unit * along)


class Sizes:
    def __init__(self, rows, heads, tokens, model, width, units):
        self.rows, self.heads = rows, heads
        self.ny = heads // 2
        self.nx = self.ny if rows % self.ny == 0 else 1
        self.nz = rows // self.nx
        self.tokens, self.model, self.width, self.units = tokens, model, width, units
        self.chunk = min(TILE, tokens)
        self.chunks = tokens // self.chunk
        self.sub = self.chunk // heads
        self.here = width // HEAD
        self.pairs = width // LANES
        self.tiles = (self.pairs + 1) // 2
        self.message = self.tiles * LANES + 8
        self.cut = model // rows


class Place:
    def __init__(self, sizes):
        s = self.s = sizes
        self.row = lax.axis_index("rows")
        self.head = lax.axis_index("heads")
        self.y, self.c = self.head // 2, lax.rem(self.head, 2)
        self.x, self.z = lax.rem(self.row, s.nx), self.row // s.nx

    def other(self):
        return (self.row, self.y * 2 + 1 - self.c)

    def group(self, step):
        return lax.rem(self.y + self.s.ny - step, self.s.ny) * 2 + self.c

    def along_y(self, step):
        return (self.row, lax.rem(self.y + step, self.s.ny) * 2 + self.c)

    def along_x(self, step):
        return (self.z * self.s.nx + lax.rem(self.x + step, self.s.nx), self.head)

    def along_z(self, step):
        return (lax.rem(self.z + step, self.s.nz) * self.s.nx + self.x, self.head)

    def along_rows(self, step):
        return (lax.rem(self.row + step, self.s.rows), self.head)

    def along_heads(self, step):
        return (self.row, lax.rem(self.head + step, self.s.heads))

    def meet(self):
        barrier = pltpu.get_barrier_semaphore()
        for step in range(1, self.s.heads):
            pl.semaphore_signal(barrier, inc=1, device_id=self.along_heads(step), device_id_type=MESH)
        for step in range(1, self.s.rows):
            pl.semaphore_signal(barrier, inc=1, device_id=self.along_rows(step), device_id_type=MESH)
        pl.semaphore_wait(barrier, self.s.heads + self.s.rows - 2)


def remote(source, target, send, receive, device):
    return pltpu.make_async_remote_copy(
        src_ref=source, dst_ref=target, send_sem=send, recv_sem=receive, device_id=device, device_id_type=MESH
    )


class Gather:
    def __init__(self, place, view, send, receive, own=None):
        self.p, self.view, self.send, self.receive = place, view, send, receive
        self.own = own

    def copy(self, group, k, slot, device):
        source = self.view(group, k)
        return remote(source, self.view(group, k), self.send.at[slot, k], self.receive.at[group, k], device)

    def own_copy(self, k, slot, device):
        group = self.p.head
        source = self.view(group, k) if self.own is None else self.own(k)
        return remote(source, self.view(group, k), self.send.at[slot, k], self.receive.at[group, k], device)

    def start(self, k):
        for step in range(1, self.p.s.ny):
            self.own_copy(k, step, self.p.along_y(step)).start()
        self.own_copy(k, 0, self.p.other()).start()

    def forward(self, k):
        ny = self.p.s.ny
        for step in range(1, ny):
            group = self.p.group(step)
            self.copy(group, k, 0, self.p.along_y(step)).wait_recv()
            self.copy(group, k, ny - 1 + step, self.p.other()).start()

    def finish(self, k):
        for step in range(self.p.s.ny):
            own = self.p.group(step)
            group = own + 1 - 2 * self.p.c
            self.copy(group, k, 0, self.p.other()).wait_recv()

    def sent(self, k):
        ny = self.p.s.ny
        for step in range(ny):
            self.own_copy(k, step, self.p.other()).wait_send()
        for step in range(1, ny):
            self.copy(self.p.group(step), k, ny - 1 + step, self.p.other()).wait_send()


class Reduce:
    def __init__(self, place, parts, near, far, sems):
        self.p, self.parts, self.near, self.far = place, parts, near, far
        self.near_send, self.near_recv, self.far_send, self.far_recv = sems

    def near_copy(self, k):
        return remote(
            self.parts.at[k, 1 - self.p.c],
            self.near.at[k],
            self.near_send.at[k],
            self.near_recv.at[k],
            self.p.other(),
        )

    def far_copy(self, k, step):
        share = lax.rem(self.p.y + step, self.p.s.ny)
        return remote(
            self.near.at[k, share],
            self.far.at[step - 1, k],
            self.far_send.at[step - 1, k],
            self.far_recv.at[step - 1, k],
            self.p.along_y(step),
        )

    def start(self, k):
        self.near_copy(k).start()

    def middle(self, k):
        self.near_copy(k).wait_recv()
        for step in range(self.p.s.ny):
            share = lax.rem(self.p.y + self.p.s.ny - 1 - step, self.p.s.ny)
            self.near[k, share] = self.near[k, share] + self.parts[k, self.p.c, share]
        for step in range(1, self.p.s.ny):
            self.far_copy(k, step).start()

    def total(self, k):
        value = self.near[k, self.p.y]
        for step in range(1, self.p.s.ny):
            self.far_copy(k, step).wait_recv()
            value = value + self.far[step - 1, k]
        return value

    def near_sent(self, k):
        self.near_copy(k).wait_send()

    def far_sent(self, k):
        for step in range(1, self.p.s.ny):
            self.far_copy(k, step).wait_send()


def iota(shape, axis):
    return lax.broadcasted_iota(jnp.int32, shape, axis)


def head_lanes(width, head):
    lanes = iota((1, width), 1) // HEAD
    return (lanes == head).astype(WIDE)


def only(value, lanes):
    return (value.astype(WIDE) * lanes).astype(LOW)


def block_ones(width):
    return (iota((width, width), 0) // HEAD == iota((width, width), 1) // HEAD).astype(WIDE).astype(LOW)


def over_heads(product, ones):
    high = product.astype(LOW)
    rest = (product - high.astype(WIDE)).astype(LOW)
    return dot(high, ones) + dot(rest, ones)


def same_head():
    return iota((LANES, LANES), 0) // HEAD == iota((LANES, LANES), 1) // HEAD


def write_message(s, message, state, total, label):
    same = same_head()
    for tile in range(s.tiles):
        first = 2 * tile * LANES
        block = jnp.where(same, state[first : first + LANES, first : first + LANES], 0.0)
        if 2 * tile + 1 < s.pairs:
            second = first + LANES
            more = jnp.where(same, state[second : second + LANES, second : second + LANES], 0.0)
            block = block + pltpu.roll(more, HEAD, 1)
        message[tile * LANES : (tile + 1) * LANES, :] = block
    at = iota((8, LANES), 0)
    tail = jnp.where(at == s.pairs, label, 0.0)
    for pair in range(s.pairs):
        tail = tail + jnp.where(at == pair, total[:, pair * LANES : (pair + 1) * LANES], 0.0)
    message[s.tiles * LANES :, :] = tail


def join_messages(place, messages, state_low, first, have_first, earlier):
    s = place.s
    tail_at = s.tiles * LANES
    label = jnp.where(have_first, messages[first, tail_at + s.pairs : tail_at + s.pairs + 1, :], -1.0)

    def one(step, carry):
        block, tail = carry
        counts = (place.row - step >= 0) if earlier else (place.row - step < 0)
        here = messages[step, tail_at + s.pairs : tail_at + s.pairs + 1, :]
        weight = jnp.where(counts, (here == label).astype(WIDE), 0.0)
        return (
            block + messages[step, 0:tail_at, :] * weight,
            tail + messages[step, tail_at : tail_at + 8, :] * weight,
        )

    start = (jnp.zeros((tail_at, LANES), WIDE), jnp.zeros((8, LANES), WIDE))
    block, tail = lax.fori_loop(1, s.rows, one, start)
    same = same_head()
    state_low[...] = jnp.zeros_like(state_low)
    for tile in range(s.tiles):
        part = block[tile * LANES : (tile + 1) * LANES]
        first_at = 2 * tile * LANES
        state_low[first_at : first_at + LANES, first_at : first_at + LANES] = jnp.where(same, part, 0.0).astype(LOW)
        if 2 * tile + 1 < s.pairs:
            at = first_at + LANES
            more = pltpu.roll(jnp.where(same, 0.0, part), HEAD, 1)
            state_low[at : at + LANES, at : at + LANES] = more.astype(LOW)
    total = jnp.concatenate([tail[pair : pair + 1] for pair in range(s.pairs)], axis=1)
    return total, label[:, 0:1]


def send_messages(place, messages, send, receive):
    for step in range(1, place.s.rows):
        remote(
            messages.at[0], messages.at[step], send.at[step], receive.at[step], place.along_rows(step)
        ).start()


def take_messages(place, messages, send, receive):
    for step in range(1, place.s.rows):
        copy = remote(messages.at[0], messages.at[step], send.at[step], receive.at[step], place.along_rows(step))
        copy.wait()


def block_mask(s, labels_down, labels_across, i, j, turned):
    shape = (s.chunk, s.chunk)
    down, across = iota(shape, 0), iota(shape, 1)
    if turned:
        ordered = (i * s.chunk + across) >= (j * s.chunk + down)
        equal = labels_down[chunk_rows(s, j), :] == labels_across[i]
    else:
        ordered = (i * s.chunk + down) >= (j * s.chunk + across)
        equal = labels_down[chunk_rows(s, i), :] == labels_across[j]
    return jnp.where(ordered & equal, 1.0, 0.0)


def chunk_rows(s, k):
    return pl.ds(pl.multiple_of(k * s.chunk, s.chunk), s.chunk)


def forward_kernel(
    s,
    pixels,
    labels_down,
    labels_across,
    first_gain,
    query_weight,
    key_weight,
    value_weight,
    out_weight,
    second_gain,
    up_weight,
    down_weight,
    cotangent,
    normed,
    query_feature,
    key_feature,
    values,
    attended,
    denominator,
    key_sum,
    hidden_low,
    hidden_share,
    gradient_share,
    pixel_share,
    gain_part,
    prefix_low,
    latest,
    middle,
    wide_gradient,
    gathered,
    weight_wide,
    weight_full,
    joined,
    hidden,
    normed_again,
    upward_low,
    low_wide,
    parts,
    near,
    far,
    messages,
    state,
    total,
    ones,
    staging,
    weight_send,
    weight_recv,
    att_send,
    att_recv,
    low_send,
    low_recv,
    message_send,
    message_recv,
    near_send,
    near_recv,
    far_send,
    far_recv,
    staging_sem,
):
    p = Place(s)
    weight_wide[p.head, 0] = out_weight[...].astype(WIDE)
    p.meet()
    weights = Gather(p, lambda g, k: weight_wide.at[g, k], weight_send, weight_recv)
    weights.start(0)

    last = labels_across[s.chunks - 1][:, s.chunk - 1 : s.chunk]
    state[...] = jnp.zeros_like(state)
    total[...] = jnp.zeros_like(total)
    ones[...] = block_ones(s.width)

    @pl.loop(0, s.chunks)
    def _(k):
        at = chunk_rows(s, k)
        unit, scale = normalise(pixels[k].reshape(s.chunk, s.model).astype(WIDE))
        low = (unit * first_gain[...]).astype(LOW)
        normed[at, :] = low
        for weight, out in ((query_weight, query_feature), (key_weight, key_feature)):
            raw = dot(low, weight[...])
            out[at, :] = jnp.where(raw > 0, raw + 1.0, jnp.exp(jnp.minimum(raw, 0.0))).astype(LOW)
        values[at, :] = dot(low, value_weight[...]).astype(LOW)
        ending = (labels_down[at, :] == last).astype(WIDE)
        kept = key_feature[at, :].astype(WIDE) * ending
        state[...] += dot_left(kept.astype(LOW), values[at, :])
        total[0:1, :] += jnp.sum(kept, axis=0, keepdims=True)

    write_message(s, messages.at[0], state, total[0:1, :], last)
    send_messages(p, messages, message_send, message_recv)

    @pl.loop(0, s.chunks)
    def _(i):
        at = chunk_rows(s, i)
        attended[at, :] = jnp.zeros((s.chunk, s.width), WIDE)
        key_sum[at, :] = jnp.zeros((s.chunk, s.width), WIDE)

        def over(j, carry):
            to = chunk_rows(s, j)
            mask = block_mask(s, labels_down, labels_across, i, j, False)
            key_sum[at, :] += dot(mask.astype(LOW), key_feature[to, :])
            numerator = attended[at, :]
            for head in range(s.here):
                lanes = head_lanes(s.width, head)
                scores = dot_right(only(query_feature[at, :], lanes), key_feature[to, :])
                numerator = numerator + dot((scores * mask).astype(LOW), only(values[to, :], lanes))
            attended[at, :] = numerator
            return carry

        lax.fori_loop(0, i + 1, over, 0)

    take_messages(p, messages, message_send, message_recv)
    prefix_total, label = join_messages(p, messages, prefix_low, 1, p.row > 0, True)
    latest[...] = jnp.broadcast_to(label, latest.shape)

    attention = Gather(p, lambda g, k: gathered.at[g, k], att_send, att_recv)

    @pl.loop(0, s.chunks)
    def _(i):
        at = chunk_rows(s, i)
        matching = (labels_down[at, :] == latest[0:1, 0:1]).astype(WIDE)
        query = query_feature[at, :].astype(WIDE)
        numerator = attended[at, :] + dot((query * matching).astype(LOW), prefix_low[...])
        sums = key_sum[at, :] + matching * prefix_total
        key_sum[at, :] = sums
        below = over_heads(query * sums, ones[...])
        denominator[at, :] = below
        value = numerator / below
        attended[at, :] = value
        gathered[p.head, i] = value.astype(LOW).astype(WIDE)
        attention.start(i)

    weights.forward(0)
    attention.forward(0)
    weights.finish(0)
    weights.sent(0)
    for group in range(s.heads):
        weight_full[group * s.width : (group + 1) * s.width, :] = weight_wide[group, 0].astype(LOW)

    hidden_gather = Gather(p, lambda g, k: low_wide.at[k, lax.rem(g, 2), g // 2], low_send, low_recv)
    reduced = Reduce(p, parts, near, far, (near_send, near_recv, far_send, far_recv))
    gain_part[...] = jnp.zeros_like(gain_part)

    def feed_forward(k):
        at = chunk_rows(s, k)
        attention.finish(k)
        for group in range(s.heads):
            joined[:, group * s.width : (group + 1) * s.width] = gathered[group, k].astype(LOW)
        shares = (2, s.ny, s.sub, TILE)
        for tile in range(s.model // TILE):
            cols = slice(tile * TILE, (tile + 1) * TILE)
            product = dot(joined[...], weight_full[:, cols])
            hidden[:, :, :, cols] = product.reshape(shares) + pixels[k, :, :, :, cols].astype(WIDE)
        hidden_share[k] = hidden[p.c, p.y]
        unit, scale = normalise(hidden[...].reshape(s.chunk, s.model))
        normed_again[at, :] = (unit * second_gain[...]).astype(LOW)

        @pl.when(k + 1 < s.chunks)
        def _():
            attention.forward(k + 1)

        low = normed_again[at, :]
        back = cotangent[k].reshape(s.chunk, s.model)
        for tile in range(s.units // TILE):
            cols = slice(tile * TILE, (tile + 1) * TILE)
            upward = dot(low, up_weight[:, cols])
            middle_back = dot_right(back, down_weight[cols, :])
            root = math.sqrt(2.0 / math.pi)
            square = upward * upward
            bent = jnp.tanh(root * upward * (1.0 + 0.044715 * square))
            half = 0.5 + 0.5 * bent
            slope = half + 0.5 * upward * (1.0 - bent * bent) * (root * (1.0 + 3.0 * 0.044715 * square))
            middle[at, cols] = (upward * half).astype(LOW)
            upward_low[at, cols] = (middle_back * slope).astype(LOW)
        low = upward_low[at, :]
        for tile in range(s.model // TILE):
            cols = slice(tile * TILE, (tile + 1) * TILE)
            parts[k, :, :, :, cols] = dot_right(low, up_weight[cols, :]).reshape(shares)
        reduced.start(k)

    def second_norm_back(k):
        grad = reduced.total(k)
        unit, scale = normalise(hidden_share[k])
        gain_part[0:1, :] += jnp.sum(grad * unit, axis=0, keepdims=True)
        part = normalise_back(unit, scale, second_gain[...], grad)
        value = cotangent[k, p.c, p.y].astype(WIDE) + part
        gradient_share[k] = value
        low_wide[k, p.c, p.y] = value.astype(LOW).astype(WIDE)
        hidden_gather.start(k)

    def staged(piece, job):
        return pltpu.make_async_copy(staging.at[job], wide_gradient.at[job, piece], staging_sem.at[job])

    def outer(job, left, right):
        for piece in range(s.nz):
            block = left(slice(piece * s.model // s.nz, (piece + 1) * s.model // s.nz))
            if piece > 0:
                staged(piece - 1, job).wait()
            for tile in range(s.units // TILE):
                cols = slice(tile * TILE, (tile + 1) * TILE)
                staging[job, :, :, cols] = dot_left(block, right[:, cols]).reshape(s.nx, s.cut, TILE)
            staged(piece, job).start()

    @pl.loop(0, s.chunks + 3)
    def _(k):
        @pl.when(k < s.chunks)
        def _():
            feed_forward(k)

        @pl.when((k >= 1) & (k <= s.chunks))
        def _():
            reduced.middle(k - 1)

        @pl.when(k == s.chunks)
        def _():
            outer(0, lambda cols: normed_again[:, cols], upward_low)

        @pl.when((k >= 2) & (k <= s.chunks + 1))
        def _():
            second_norm_back(k - 2)

        @pl.when(k == s.chunks + 1)
        def _():
            outer(1, lambda cols: cotangent_rows(s, cotangent, cols), middle)

        @pl.when((k >= 3) & (k <= s.chunks + 2))
        def _():
            hidden_gather.forward(k - 3)

    for k in range(s.chunks):
        pixel_share[k] = pixels[k, p.c, p.y]
        hidden_gather.finish(k)
        hidden_low[k * s.chunk : (k + 1) * s.chunk, :] = low_wide[k].reshape(s.chunk, s.model).astype(LOW)
    for job in range(2):
        staged(s.nz - 1, job).wait()
    for k in range(s.chunks):
        attention.sent(k)
        hidden_gather.sent(k)
        reduced.near_sent(k)
        reduced.far_sent(k)


def cotangent_rows(s, cotangent, cols):
    return cotangent[:, :, :, :, cols].reshape(s.tokens, cols.stop - cols.start)


class Scatter:
    def __init__(self, place, source, near, far, sems):
        self.p, self.source, self.near, self.far = place, source, near, far
        self.near_send, self.near_recv, self.far_send, self.far_recv = sems

    def piece(self, turn):
        return lax.rem(self.p.z + turn + 1, self.p.s.nz)

    def near_copy(self, turn, step):
        to = lax.rem(self.p.x + step, self.p.s.nx)
        return remote(
            self.source.at[self.piece(turn), to],
            self.near.at[step - 1, turn],
            self.near_send.at[step - 1, turn],
            self.near_recv.at[step - 1, turn],
            self.p.along_x(step),
        )

    def far_copy(self, turn):
        return remote(
            self.near.at[0, turn],
            self.far.at[turn],
            self.far_send.at[turn],
            self.far_recv.at[turn],
            self.p.along_z(turn + 1),
        )

    def start(self, turn):
        for step in range(1, self.p.s.nx):
            self.near_copy(turn, step).start()

    def middle(self, turn, own):
        value = own
        for step in range(1, self.p.s.nx):
            self.near_copy(turn, step).wait_recv()
            value = value + self.near[step - 1, turn]
        self.near[0, turn] = value
        if turn < self.p.s.nz - 1:
            self.far_copy(turn).start()

    def total(self):
        value = self.near[0, self.p.s.nz - 1]
        for turn in range(self.p.s.nz - 1):
            self.far_copy(turn).wait_recv()
            value = value + self.far[turn]
        return value

    def sent(self):
        for turn in range(self.p.s.nz):
            for step in range(1, self.p.s.nx):
                self.near_copy(turn, step).wait_send()
        for turn in range(self.p.s.nz - 1):
            self.far_copy(turn).wait_send()


def backward_kernel(
    s,
    labels_down,
    labels_across,
    normed,
    query_feature,
    key_feature,
    values,
    attended,
    denominator,
    key_sum,
    hidden_low,
    hidden_share,
    gradient_share,
    pixel_share,
    gain_part,
    prefix_low,
    latest,
    middle,
    down_weight,
    query_weight,
    key_weight,
    value_weight,
    out_weight,
    first_gain,
    wide_gradient,
    result,
    gains,
    up_out,
    down_out,
    narrow_out,
    pixel_gradient,
    result_wide,
    parts,
    near_two,
    far_two,
    near_four,
    far_four,
    result_own,
    pixel_own,
    numerator_low,
    denominator_back,
    spread_back,
    query_back,
    key_back,
    value_back,
    narrow_low,
    suffix_low,
    state,
    total,
    ones,
    messages,
    narrow_gradient,
    own_wide,
    near_up,
    far_up,
    near_down,
    far_down,
    near_narrow,
    far_narrow,
    gain_heads,
    gain_x,
    gain_z,
    message_send,
    message_recv,
    two_near_send,
    two_near_recv,
    two_far_send,
    two_far_recv,
    four_near_send,
    four_near_recv,
    four_far_send,
    four_far_recv,
    result_send,
    result_recv,
    pixel_send,
    pixel_recv,
    scatter_near_send,
    scatter_near_recv,
    scatter_far_send,
    scatter_far_recv,
    gain_send,
    gain_recv,
    own_sem,
    result_sem,
    pixel_sem,
    read_sem,
):
    p = Place(s)
    p.meet()

    def scatter(job, source, near, far):
        sems = (
            scatter_near_send.at[job],
            scatter_near_recv.at[job],
            scatter_far_send.at[job],
            scatter_far_recv.at[job],
        )
        return Scatter(p, source, near, far, sems)

    up = scatter(0, wide_gradient.at[0], near_up, far_up)
    down = scatter(1, wide_gradient.at[1], near_down, far_down)
    narrow = scatter(2, narrow_gradient, near_narrow, far_narrow)
    for job in (up, down):
        for turn in range(s.nz):
            job.start(turn)

    wide_jobs = (up, down)

    def own_load(at):
        job, turn = at // s.nz, at % s.nz
        source = wide_gradient.at[job, wide_jobs[job].piece(turn), p.x]
        return pltpu.make_async_copy(source, own_wide.at[at % 2], own_sem.at[at % 2])

    def wide_middle(at):
        own_load(at).wait()
        wide_jobs[at // s.nz].middle(at % s.nz, own_wide[at % 2])
        if at + 2 < 2 * s.nz:
            own_load(at + 2).start()

    own_load(0).start()
    own_load(1).start()
    two = Reduce(p, parts, near_two, far_two, (two_near_send, two_near_recv, two_far_send, two_far_recv))
    four = Reduce(p, parts, near_four, far_four, (four_near_send, four_near_recv, four_far_send, four_far_recv))
    result_gather = Gather(
        p,
        lambda g, k: result_wide.at[k, lax.rem(g, 2), g // 2],
        result_send,
        result_recv,
        lambda k: result_own.at[k],
    )
    pixel_gather = Gather(
        p,
        lambda g, k: pixel_gradient.at[k, lax.rem(g, 2), g // 2],
        pixel_send,
        pixel_recv,
        lambda k: pixel_own.at[k],
    )
    shares = (2, s.ny, s.sub, TILE)

    @pl.loop(0, s.chunks)
    def _(k):
        low = middle[chunk_rows(s, k), :]
        for tile in range(s.model // TILE):
            cols = slice(tile * TILE, (tile + 1) * TILE)
            parts[k, :, :, :, cols] = dot(low, down_weight[:, cols]).reshape(shares)
        two.start(k)

    first = labels_across[0][:, 0:1]
    state[...] = jnp.zeros_like(state)
    total[...] = jnp.zeros_like(total)
    ones[...] = block_ones(s.width)

    @pl.loop(0, s.chunks)
    def _(k):
        at = chunk_rows(s, k)
        back = dot_right(hidden_low[at, :], out_weight[...])
        below = denominator[at, :]
        low = (back / below).astype(LOW)
        numerator_low[at, :] = low
        slope = -over_heads(back * attended[at, :], ones[...]) / below
        denominator_back[at, :] = slope
        query = query_feature[at, :].astype(WIDE)
        spread = slope * query
        spread_back[at, :] = spread.astype(LOW)
        leading = (labels_down[at, :] == first).astype(WIDE)
        state[...] += dot_left((query * leading).astype(LOW), low)
        total[0:1, :] += jnp.sum(spread * leading, axis=0, keepdims=True)

    write_message(s, messages.at[0], state, total[0:1, :], first)
    send_messages(p, messages, message_send, message_recv)

    @pl.loop(0, s.chunks)
    def _(k):
        two.middle(k)

    wide_middle(0)

    @pl.loop(0, s.chunks)
    def _(i):
        at = chunk_rows(s, i)
        query_back[at, :] = denominator_back[at, :] * key_sum[at, :]

        def over(j, carry):
            to = chunk_rows(s, j)
            mask = block_mask(s, labels_down, labels_across, i, j, False)
            value = query_back[at, :]
            for head in range(s.here):
                lanes = head_lanes(s.width, head)
                scores = dot_right(only(numerator_low[at, :], lanes), values[to, :])
                value = value + dot((scores * mask).astype(LOW), only(key_feature[to, :], lanes))
            query_back[at, :] = value
            return carry

        lax.fori_loop(0, i + 1, over, 0)

    wide_middle(1)

    @pl.loop(0, s.chunks)
    def _(j):
        to = chunk_rows(s, j)
        key_back[to, :] = jnp.zeros((s.chunk, s.width), WIDE)
        value_back[to, :] = jnp.zeros((s.chunk, s.width), WIDE)

        def over(i, carry):
            at = chunk_rows(s, i)
            mask = block_mask(s, labels_down, labels_across, i, j, True)
            key_value = key_back[to, :] + dot(mask.astype(LOW), spread_back[at, :])
            value_value = value_back[to, :]
            for head in range(s.here):
                lanes = head_lanes(s.width, head)
                back = dot_right(only(values[to, :], lanes), numerator_low[at, :])
                key_value = key_value + dot((back * mask).astype(LOW), only(query_feature[at, :], lanes))
                scores = dot_right(only(key_feature[to, :], lanes), query_feature[at, :])
                value_value = value_value + dot((scores * mask).astype(LOW), only(numerator_low[at, :], lanes))
            key_back[to, :] = key_value
            value_back[to, :] = value_value
            return carry

        lax.fori_loop(j, s.chunks, over, 0)

    @pl.loop(0, s.chunks)
    def _(k):
        result_own[k] = (hidden_share[k] + two.total(k)).astype(LOW).astype(WIDE)
        result_gather.start(k)

    take_messages(p, messages, message_send, message_recv)
    suffix_total, label = join_messages(p, messages, suffix_low, s.rows - 1, p.row < s.rows - 1, False)
    following = label

    @pl.loop(0, s.chunks)
    def _(k):
        at = chunk_rows(s, k)
        matching = (labels_down[at, :] == latest[0:1, 0:1]).astype(WIDE)
        later = (labels_down[at, :] == following).astype(WIDE)
        query, key = query_feature[at, :], key_feature[at, :]
        value = query_back[at, :] + matching * dot_right(numerator_low[at, :], prefix_low[...])
        low = (value * jnp.minimum(query.astype(WIDE), 1.0)).astype(LOW)
        numerator_value = value_back[at, :] + later * dot(key, suffix_low[...])
        key_value = key_back[at, :] + later * (dot_right(values[at, :], suffix_low[...]) + suffix_total)
        key_low = (key_value * jnp.minimum(key.astype(WIDE), 1.0)).astype(LOW)
        value_low = numerator_value.astype(LOW)
        narrow_low[0, at, :] = low
        narrow_low[1, at, :] = key_low
        narrow_low[2, at, :] = value_low
        two.near_sent(k)
        for tile in range(s.model // TILE):
            cols = slice(tile * TILE, (tile + 1) * TILE)
            product = (
                dot_right(low, query_weight[cols, :])
                + dot_right(key_low, key_weight[cols, :])
                + dot_right(value_low, value_weight[cols, :])
            )
            parts[k, :, :, :, cols] = product.reshape(shares)
        four.start(k)

    wide_middle(2)
    span = s.nx * s.cut
    for piece in range(s.nz):
        cols = slice(piece * span, (piece + 1) * span)
        shape = (s.nx, s.cut, s.width)
        product = dot_left(hidden_low[:, cols], attended[...].astype(LOW))
        narrow_gradient[piece, :, :, 0 : s.width] = product.reshape(shape)
        for part in range(3):
            product = dot_left(normed[:, cols], narrow_low[part])
            narrow_gradient[piece, :, :, (part + 1) * s.width : (part + 2) * s.width] = product.reshape(shape)
    for turn in range(s.nz):
        narrow.start(turn)

    @pl.loop(0, s.chunks)
    def _(k):
        four.middle(k)

    for at in range(3, s.nz):
        wide_middle(at)
    gain_heads[0] = gain_part[...]

    def result_local(k):
        return pltpu.make_async_copy(result_own.at[k], result_wide.at[k, p.c, p.y], result_sem.at[k])

    def pixel_local(k):
        return pltpu.make_async_copy(pixel_own.at[k], pixel_gradient.at[k, p.c, p.y], pixel_sem.at[k])

    def result_read(k):
        return pltpu.make_async_copy(result_wide.at[k], parts.at[k], read_sem.at[k])

    @pl.loop(0, s.chunks)
    def _(k):
        grad = four.total(k)
        unit, scale = normalise(pixel_share[k].astype(WIDE))
        gain_heads[0, 1:2, :] += jnp.sum(grad * unit, axis=0, keepdims=True)
        pixel_own[k] = gradient_share[k] + normalise_back(unit, scale, first_gain[...], grad)
        pixel_gather.start(k)
        pixel_local(k).start()
        result_local(k).start()

    wide_middle(s.nz)

    def gain_round(buffer, device, index):
        copies = []
        for step in range(1, buffer.shape[0]):
            copy = remote(
                buffer.at[0], buffer.at[step], gain_send.at[index, step], gain_recv.at[index, step], device(step)
            )
            copy.start()
            copies.append(copy)
        for copy in copies:
            copy.wait()
        value = buffer[0]
        for step in range(1, buffer.shape[0]):
            value = value + buffer[step]
        return value

    gain_x[0] = gain_round(gain_heads, p.along_heads, 0)
    gain_z[0] = gain_round(gain_x, p.along_x, 1)
    gains[...] = gain_round(gain_z, p.along_z, 2)

    for at in range(s.nz + 1, 2 * s.nz):
        wide_middle(at)
    for k in range(s.chunks):
        result_gather.forward(k)
    for k in range(s.chunks):
        pixel_gather.forward(k)
    for k in range(s.chunks):
        result_gather.finish(k)
        result_local(k).wait()
        four.near_sent(k)
        result_read(k).start()
    for k in range(s.chunks):
        result_read(k).wait()
        result[k * s.chunk : (k + 1) * s.chunk, :] = parts[k].reshape(s.chunk, s.model).astype(LOW)
    up_out[...] = up.total()
    for turn in range(s.nz):
        narrow.middle(turn, narrow_gradient[narrow.piece(turn), p.x])
    down_out[...] = down.total()
    for k in range(s.chunks):
        pixel_gather.finish(k)
        pixel_local(k).wait()
        pixel_gather.sent(k)
        result_gather.sent(k)
        two.far_sent(k)
        four.far_sent(k)
    narrow_out[...] = narrow.total()
    for job in (up, down, narrow):
        job.sent()


def vmem(count):
    return [pl.BlockSpec(memory_space=pltpu.VMEM)] * count


def dma(*shape):
    return pltpu.SemaphoreType.DMA(shape)


def on_device(
    rows,
    heads,
    pixels,
    crop_ids,
    first_gain,
    query_weight,
    key_weight,
    value_weight,
    out_weight,
    second_gain,
    up_weight,
    down_weight,
    cotangent,
):
    tokens, model = pixels.shape
    s = Sizes(rows, heads, tokens, model, query_weight.shape[1], up_weight.shape[1])
    whole = (s.chunks, 2, s.ny, s.sub, model)
    share = (s.chunks, s.sub, model)
    labels = crop_ids.astype(WIDE)
    labels_down = labels.reshape(tokens, 1)
    labels_across = labels.reshape(s.chunks, 1, s.chunk)
    shape = jax.ShapeDtypeStruct
    any_space = pl.BlockSpec(memory_space=pl.ANY)

    def reduce_sems():
        return [
            dma(s.chunks),
            dma(s.chunks),
            dma(s.ny - 1, s.chunks),
            dma(s.ny - 1, s.chunks),
        ]

    def gather_sems(count):
        return [dma(2 * s.ny - 1, count), dma(heads, count)]

    outs = [
        shape((tokens, model), LOW),
        shape((tokens, s.width), LOW),
        shape((tokens, s.width), LOW),
        shape((tokens, s.width), LOW),
        shape((tokens, s.width), WIDE),
        shape((tokens, s.width), WIDE),
        shape((tokens, s.width), WIDE),
        shape((tokens, model), LOW),
        shape(share, WIDE),
        shape(share, WIDE),
        shape(share, LOW),
        shape((8, model), WIDE),
        shape((s.width, s.width), LOW),
        shape((8, LANES), WIDE),
        shape((tokens, s.units), LOW),
        shape((2, s.nz, s.nx, s.cut, s.units), WIDE),
    ]
    (
        normed,
        query_feature,
        key_feature,
        values,
        attended,
        denominator,
        key_sum,
        hidden_low,
        hidden_share,
        gradient_share,
        pixel_share,
        gain_part,
        prefix_low,
        latest,
        middle,
        wide_gradient,
    ) = pl.pallas_call(
        functools.partial(forward_kernel, s),
        out_shape=outs,
        in_specs=vmem(12),
        out_specs=vmem(15) + [any_space],
        scratch_shapes=[
            pltpu.VMEM((heads, s.chunks, s.chunk, s.width), WIDE),
            pltpu.VMEM((heads, 1, s.width, model), WIDE),
            pltpu.VMEM((model, model), LOW),
            pltpu.VMEM((s.chunk, model), LOW),
            pltpu.VMEM(whole[1:], WIDE),
            pltpu.VMEM((tokens, model), LOW),
            pltpu.VMEM((tokens, s.units), LOW),
            pltpu.VMEM(whole, WIDE),
            pltpu.VMEM(whole, WIDE),
            pltpu.VMEM((s.chunks, s.ny, s.sub, model), WIDE),
            pltpu.VMEM((s.ny - 1,) + share, WIDE),
            pltpu.VMEM((rows, s.message, LANES), WIDE),
            pltpu.VMEM((s.width, s.width), WIDE),
            pltpu.VMEM((8, s.width), WIDE),
            pltpu.VMEM((s.width, s.width), LOW),
            pltpu.VMEM((2, s.nx, s.cut, s.units), WIDE),
            *gather_sems(1),
            *gather_sems(s.chunks),
            *gather_sems(s.chunks),
            dma(rows),
            dma(rows),
            *reduce_sems(),
            dma(2),
        ],
        compiler_params=pltpu.CompilerParams(
            collective_id=0, has_side_effects=True, vmem_limit_bytes=60 << 20
        ),
        name="forward_part",
    )(
        pixels.reshape(whole),
        labels_down,
        labels_across,
        first_gain.reshape(1, model),
        query_weight,
        key_weight,
        value_weight,
        out_weight,
        second_gain.reshape(1, model),
        up_weight,
        down_weight,
        cotangent.reshape(whole),
    )
    columns = 4 * s.width
    outs = [
        shape((tokens, model), LOW),
        shape((8, model), WIDE),
        shape((s.cut, s.units), WIDE),
        shape((s.cut, s.units), WIDE),
        shape((s.cut, columns), WIDE),
        shape(whole, WIDE),
        shape(whole, WIDE),
    ]

    def scatter_buffers(width):
        return [
            pltpu.VMEM((s.nx - 1, s.nz, s.cut, width), WIDE),
            pltpu.VMEM((s.nz - 1, s.cut, width), WIDE),
        ]

    def reduce_buffers():
        return [
            pltpu.VMEM((s.chunks, s.ny, s.sub, model), WIDE),
            pltpu.VMEM((s.ny - 1,) + share, WIDE),
        ]

    result, gains, up_out, down_out, narrow_out, pixel_gradient, unused = pl.pallas_call(
        functools.partial(backward_kernel, s),
        out_shape=outs,
        in_specs=vmem(23) + [any_space],
        out_specs=vmem(5) + [any_space] * 2,
        scratch_shapes=[
            pltpu.VMEM(whole, WIDE),
            *reduce_buffers(),
            *reduce_buffers(),
            pltpu.VMEM(share, WIDE),
            pltpu.VMEM(share, WIDE),
            pltpu.VMEM((tokens, s.width), LOW),
            pltpu.VMEM((tokens, s.width), WIDE),
            pltpu.VMEM((tokens, s.width), LOW),
            pltpu.VMEM((tokens, s.width), WIDE),
            pltpu.VMEM((tokens, s.width), WIDE),
            pltpu.VMEM((tokens, s.width), WIDE),
            pltpu.VMEM((3, tokens, s.width), LOW),
            pltpu.VMEM((s.width, s.width), LOW),
            pltpu.VMEM((s.width, s.width), WIDE),
            pltpu.VMEM((8, s.width), WIDE),
            pltpu.VMEM((s.width, s.width), LOW),
            pltpu.VMEM((rows, s.message, LANES), WIDE),
            pltpu.VMEM((s.nz, s.nx, s.cut, columns), WIDE),
            pltpu.VMEM((2, s.cut, s.units), WIDE),
            *scatter_buffers(s.units),
            *scatter_buffers(s.units),
            *scatter_buffers(columns),
            pltpu.VMEM((heads, 8, model), WIDE),
            pltpu.VMEM((s.nx, 8, model), WIDE),
            pltpu.VMEM((s.nz, 8, model), WIDE),
            dma(rows),
            dma(rows),
            *reduce_sems(),
            *reduce_sems(),
            *gather_sems(s.chunks),
            *gather_sems(s.chunks),
            dma(3, s.nx - 1, s.nz),
            dma(3, s.nx - 1, s.nz),
            dma(3, s.nz - 1),
            dma(3, s.nz - 1),
            dma(3, max(heads, s.nx, s.nz)),
            dma(3, max(heads, s.nx, s.nz)),
            dma(2),
            dma(s.chunks),
            dma(s.chunks),
            dma(s.chunks),
        ],
        compiler_params=pltpu.CompilerParams(
            collective_id=1, has_side_effects=True, vmem_limit_bytes=60 << 20
        ),
        name="backward_part",
    )(
        labels_down,
        labels_across,
        normed,
        query_feature,
        key_feature,
        values,
        attended,
        denominator,
        key_sum,
        hidden_low,
        hidden_share,
        gradient_share,
        pixel_share,
        gain_part,
        prefix_low,
        latest,
        middle,
        down_weight,
        query_weight,
        key_weight,
        value_weight,
        out_weight,
        first_gain.reshape(1, model),
        wide_gradient,
    )
    start = lax.axis_index("rows") * s.cut
    second_part, first_part = (lax.dynamic_slice(gains[i], (start,), (s.cut,)) for i in range(2))
    narrow = [narrow_out[:, i * s.width : (i + 1) * s.width] for i in range(4)]
    return (
        result,
        pixel_gradient.reshape(tokens, model),
        first_part,
        narrow[1],
        narrow[2],
        narrow[3],
        narrow[0].T,
        second_part,
        up_out,
        down_out.T,
    )


def solution(mesh):
    return jax.shard_map(
        functools.partial(on_device, mesh.shape["rows"], mesh.shape["heads"]),
        mesh=mesh,
        in_specs=(
            P("rows", None),
            P("rows"),
            P(),
            P(None, "heads"),
            P(None, "heads"),
            P(None, "heads"),
            P("heads", None),
            P(),
            P(None, "heads"),
            P("heads", None),
            P("rows", None),
        ),
        out_specs=(
            P("rows", None),
            P("rows", None),
            P("rows"),
            P("rows", "heads"),
            P("rows", "heads"),
            P("rows", "heads"),
            P("heads", "rows"),
            P("rows"),
            P("rows", "heads"),
            P("heads", "rows"),
        ),
        check_vma=False,
    )
```

time: 1070 us -> 371 us (0.35)
  the two profiles are of different devices: /device:TPU:0 before, /device:TPU:15 now
where the time goes in v1:
time: 371 us
  Pallas kernels  357 us (96%)
  local copies, waits for them, and re-layouts  12.9 us (3%)
    pallas_call x1, Pallas kernels, on_device(): pl.pallas_call(functools.partial(backward_kernel, s), out_shape=outs, in_...  251 us
    pallas_call x1, Pallas kernels, on_device(): pl.pallas_call(functools.partial(forward_kernel, s), out_shape=outs, in_s...  105 us
    unnamed x13, local copies, waits for them, and re-layouts  8.55 us

profile of v1, /device:TPU:15, one launch (start us, length us, event | category | flops | bytes accessed | tf_op | source)
XLA Modules:
  0.0 370.8 jit_solution(18018373838253474492)
XLA Ops:
  0.6 0.7 convert_element_type.3
  1.3 0.0 copy-start.3
  1.3 1.0 copy.24.labels_down
  2.4 0.0 copy-done.3
  2.4 105.3 %forward_part.1 = (bf16[1024,1024]{1,0:T(8,128)(2,1)}, bf16[1024,256]{1,0:T(8,128)(2,1)}, bf16[1024,256]{1,0:T(8,128)(2,1)}, bf16[1024,256]{1,0:T(8,128)(2,1)}, ...) custom-call(bf16[4,2,2,64,1024]{4,3,2,1,0:T(8,128)(2,1)} %bitcast.15, ...), custom_call_target="tpu_custom_call" | custom-call | tf_op jit(solution)/shard_map/forward_part/pallas_call | solution.py:1026
  107.7 251.2 %backward_part.1 = (bf16[1024,1024]{1,0:T(8,128)(2,1)}, f32[8,1024]{1,0:T(8,128)}, f32[128,1024]{1,0:T(8,128)}, f32[128,1024]{1,0:T(8,128)}, f32[128,1024]{1,0:T...) custom-call(f32[1024,1]{1,0:T(8,128)} %copy.24.labels_down, f32[4,1,256]{2,1,0:T(1,128)} %bitcast.20, ...), custom_call_target="tpu_custom_call" | custom-call | tf_op jit(solution)/shard_map/backward_part/pallas_call | solution.py:1097
  358.9 0.0 copy-start.1
  358.9 0.9 fusion
  359.9 0.5 dynamic-slice_bitcast_fusion
  360.4 1.8 slice_bitcast_fusion
  362.2 0.8 copy.25
  363.0 2.0 copy.26
  365.0 0.0 copy-done.1
  365.0 0.0 copy-start
  365.0 1.3 copy.30
  366.3 1.6 copy-done
  368.0 0.0 copy-start.2
  368.0 2.0 copy.31
  370.0 0.0 copy-done.2
  370.0 0.8 copy.32
Async XLA Ops:
  1.3 1.0 copy-start.3
  358.9 6.1 %copy-start.1 = (bf16[1024,1024]{1,0:T(8,128)(2,1)S(1)}, bf16[1024,1024]{1,0:T(8,128)(2,1)}, u32[]{:S(2)}) copy-start(bf16[1024,1024]{1,0:T(8,128)(2,1)} %get-tuple-element.92) | copy-start | bytes 6291460
  365.0 2.9 copy-start
  368.0 2.0 copy-start.2

commit v2 on v1

--- a/solution.py
+++ b/solution.py
@@ -15,6 +15,7 @@
 WIDE = jnp.float32
 LANES = 128
 TILE = 256
+AHEAD = 3
 
 
 def dot(left, right):
@@ -700,23 +701,33 @@
     up = scatter(0, wide_gradient.at[0], near_up, far_up)
     down = scatter(1, wide_gradient.at[1], near_down, far_down)
     narrow = scatter(2, narrow_gradient, near_narrow, far_narrow)
-    for job in (up, down):
-        for turn in range(s.nz):
-            job.start(turn)
-
-    wide_jobs = (up, down)
+    jobs = (up, down, narrow)
+    wide = 2 * s.nz
+    flight = {"next": 0, "ready": wide}
+
+    def push(limit):
+        while flight["next"] <= limit and flight["next"] < flight["ready"]:
+            at = flight["next"]
+            jobs[at // s.nz].start(at % s.nz)
+            flight["next"] = at + 1
 
     def own_load(at):
         job, turn = at // s.nz, at % s.nz
-        source = wide_gradient.at[job, wide_jobs[job].piece(turn), p.x]
+        source = wide_gradient.at[job, jobs[job].piece(turn), p.x]
         return pltpu.make_async_copy(source, own_wide.at[at % 2], own_sem.at[at % 2])
 
-    def wide_middle(at):
-        own_load(at).wait()
-        wide_jobs[at // s.nz].middle(at % s.nz, own_wide[at % 2])
-        if at + 2 < 2 * s.nz:
+    def take(at):
+        job, turn = at // s.nz, at % s.nz
+        if at < wide:
+            own_load(at).wait()
+            jobs[job].middle(turn, own_wide[at % 2])
+        else:
+            narrow.middle(turn, narrow_gradient[narrow.piece(turn), p.x])
+        if at + 2 < wide:
             own_load(at + 2).start()
-
+        push(at + AHEAD)
+
+    push(0)
     own_load(0).start()
     own_load(1).start()
     two = Reduce(p, parts, near_two, far_two, (two_near_send, two_near_recv, two_far_send, two_far_recv))
@@ -737,14 +748,6 @@
     )
     shares = (2, s.ny, s.sub, TILE)
 
-    @pl.loop(0, s.chunks)
-    def _(k):
-        low = middle[chunk_rows(s, k), :]
-        for tile in range(s.model // TILE):
-            cols = slice(tile * TILE, (tile + 1) * TILE)
-            parts[k, :, :, :, cols] = dot(low, down_weight[:, cols]).reshape(shares)
-        two.start(k)
-
     first = labels_across[0][:, 0:1]
     state[...] = jnp.zeros_like(state)
     total[...] = jnp.zeros_like(total)
@@ -768,12 +771,21 @@
 
     write_message(s, messages.at[0], state, total[0:1, :], first)
     send_messages(p, messages, message_send, message_recv)
+    push(AHEAD - 1)
+
+    @pl.loop(0, s.chunks)
+    def _(k):
+        low = middle[chunk_rows(s, k), :]
+        for tile in range(s.model // TILE):
+            cols = slice(tile * TILE, (tile + 1) * TILE)
+            parts[k, :, :, :, cols] = dot(low, down_weight[:, cols]).reshape(shares)
+        two.start(k)
 
     @pl.loop(0, s.chunks)
     def _(k):
         two.middle(k)
 
-    wide_middle(0)
+    take(0)
 
     @pl.loop(0, s.chunks)
     def _(i):
@@ -793,7 +805,7 @@
 
         lax.fori_loop(0, i + 1, over, 0)
 
-    wide_middle(1)
+    take(1)
 
     @pl.loop(0, s.chunks)
     def _(j):
@@ -853,7 +865,12 @@
             parts[k, :, :, :, cols] = product.reshape(shares)
         four.start(k)
 
-    wide_middle(2)
+
+    @pl.loop(0, s.chunks)
+    def _(k):
+        four.middle(k)
+
+    take(2)
     span = s.nx * s.cut
     for piece in range(s.nz):
         cols = slice(piece * span, (piece + 1) * span)
@@ -863,15 +880,18 @@
         for part in range(3):
             product = dot_left(normed[:, cols], narrow_low[part])
             narrow_gradient[piece, :, :, (part + 1) * s.width : (part + 2) * s.width] = product.reshape(shape)
-    for turn in range(s.nz):
-        narrow.start(turn)
-
-    @pl.loop(0, s.chunks)
-    def _(k):
-        four.middle(k)
-
-    for at in range(3, s.nz):
-        wide_middle(at)
+    flight["ready"] = 3 * s.nz
+    rest = list(range(3, 3 * s.nz))
+
+    def take_some(count):
+        for at in rest[:count]:
+            take(at)
+        del rest[:count]
+
+    def take_until_left(count):
+        take_some(max(0, len(rest) - count))
+
+    take_until_left(7)
     gain_heads[0] = gain_part[...]
 
     def result_local(k):
@@ -893,33 +913,41 @@
         pixel_local(k).start()
         result_local(k).start()
 
-    wide_middle(s.nz)
-
-    def gain_round(buffer, device, index):
-        copies = []
-        for step in range(1, buffer.shape[0]):
-            copy = remote(
-                buffer.at[0], buffer.at[step], gain_send.at[index, step], gain_recv.at[index, step], device(step)
-            )
+    def gain_copies(index, buffer, device):
+        return [
+            remote(buffer.at[0], buffer.at[step], gain_send.at[index, step], gain_recv.at[index, step], device(step))
+            for step in range(1, buffer.shape[0])
+        ]
+
+    def gain_start(*what):
+        for copy in gain_copies(*what):
             copy.start()
-            copies.append(copy)
-        for copy in copies:
+
+    def gain_total(*what):
+        for copy in gain_copies(*what):
             copy.wait()
-        value = buffer[0]
-        for step in range(1, buffer.shape[0]):
-            value = value + buffer[step]
+        value = what[1][0]
+        for step in range(1, what[1].shape[0]):
+            value = value + what[1][step]
         return value
 
-    gain_x[0] = gain_round(gain_heads, p.along_heads, 0)
-    gain_z[0] = gain_round(gain_x, p.along_x, 1)
-    gains[...] = gain_round(gain_z, p.along_z, 2)
-
-    for at in range(s.nz + 1, 2 * s.nz):
-        wide_middle(at)
+    rounds = (
+        (0, gain_heads, p.along_heads),
+        (1, gain_x, p.along_x),
+        (2, gain_z, p.along_z),
+    )
+    gain_start(*rounds[0])
+    take_until_left(5)
     for k in range(s.chunks):
         result_gather.forward(k)
+    gain_x[0] = gain_total(*rounds[0])
+    gain_start(*rounds[1])
+    take_until_left(4)
     for k in range(s.chunks):
         pixel_gather.forward(k)
+    take_until_left(3)
+    gain_z[0] = gain_total(*rounds[1])
+    gain_start(*rounds[2])
     for k in range(s.chunks):
         result_gather.finish(k)
         result_local(k).wait()
@@ -928,10 +956,10 @@
     for k in range(s.chunks):
         result_read(k).wait()
         result[k * s.chunk : (k + 1) * s.chunk, :] = parts[k].reshape(s.chunk, s.model).astype(LOW)
+    take_until_left(2)
     up_out[...] = up.total()
-    for turn in range(s.nz):
-        narrow.middle(turn, narrow_gradient[narrow.piece(turn), p.x])
-    down_out[...] = down.total()
+    gains[...] = gain_total(*rounds[2])
+    take_until_left(1)
     for k in range(s.chunks):
         pixel_gather.finish(k)
         pixel_local(k).wait()
@@ -939,8 +967,10 @@
         result_gather.sent(k)
         two.far_sent(k)
         four.far_sent(k)
+    take_until_left(0)
+    down_out[...] = down.total()
     narrow_out[...] = narrow.total()
-    for job in (up, down, narrow):
+    for job in jobs:
         job.sent()
 
 

time: 371 us -> 304 us (0.82)
  the two profiles are of different devices: /device:TPU:15 before, /device:TPU:0 now
where the time goes in v2:
time: 304 us
  Pallas kernels  289 us (95%)
  local copies, waits for them, and re-layouts  12.9 us (4%)
    pallas_call x1, Pallas kernels, on_device(): pl.pallas_call(functools.partial(backward_kernel, s), out_shape=outs, in_...  180 us
    pallas_call x1, Pallas kernels, on_device(): pl.pallas_call(functools.partial(forward_kernel, s), out_shape=outs, in_s...  109 us
    unnamed x13, local copies, waits for them, and re-layouts  8.55 us

profile of v2, /device:TPU:0, one launch (start us, length us, event | category | flops | bytes accessed | tf_op | source)
XLA Modules:
  0.0 303.6 jit_solution(15428996108664433288)
XLA Ops:
  0.6 0.7 convert_element_type.3
  1.3 0.0 copy-start.3
  1.3 1.0 copy.24.labels_down
  2.4 0.0 copy-done.3
  2.4 109.1 %forward_part.1 = (bf16[1024,1024]{1,0:T(8,128)(2,1)}, bf16[1024,256]{1,0:T(8,128)(2,1)}, bf16[1024,256]{1,0:T(8,128)(2,1)}, bf16[1024,256]{1,0:T(8,128)(2,1)}, ...) custom-call(bf16[4,2,2,64,1024]{4,3,2,1,0:T(8,128)(2,1)} %bitcast.15, ...), custom_call_target="tpu_custom_call" | custom-call | tf_op jit(solution)/shard_map/forward_part/pallas_call | solution.py:1056
  111.4 180.3 %backward_part.1 = (bf16[1024,1024]{1,0:T(8,128)(2,1)}, f32[8,1024]{1,0:T(8,128)}, f32[128,1024]{1,0:T(8,128)}, f32[128,1024]{1,0:T(8,128)}, f32[128,1024]{1,0:T...) custom-call(f32[1024,1]{1,0:T(8,128)} %copy.24.labels_down, f32[4,1,256]{2,1,0:T(1,128)} %bitcast.20, ...), custom_call_target="tpu_custom_call" | custom-call | tf_op jit(solution)/shard_map/backward_part/pallas_call | solution.py:1127
  291.7 0.0 copy-start.1
  291.7 0.9 fusion
  292.7 0.5 dynamic-slice_bitcast_fusion
  293.2 1.8 slice_bitcast_fusion
  295.0 0.8 copy.25
  295.8 2.0 copy.26
  297.8 0.0 copy-done.1
  297.8 0.0 copy-start
  297.8 1.3 copy.30
  299.2 1.6 copy-done
  300.8 0.0 copy-start.2
  300.8 2.0 copy.31
  302.8 0.0 copy-done.2
  302.8 0.8 copy.32
Async XLA Ops:
  1.3 1.0 copy-start.3
  291.7 6.1 %copy-start.1 = (bf16[1024,1024]{1,0:T(8,128)(2,1)S(1)}, bf16[1024,1024]{1,0:T(8,128)(2,1)}, u32[]{:S(2)}) copy-start(bf16[1024,1024]{1,0:T(8,128)(2,1)} %get-tuple-element.92) | copy-start | bytes 6291460
  297.8 2.9 copy-start
  300.8 2.0 copy-start.2

commit v3 on v2

--- a/solution.py
+++ b/solution.py
@@ -15,7 +15,8 @@
 WIDE = jnp.float32
 LANES = 128
 TILE = 256
-AHEAD = 3
+AHEAD = 2
+FIRST = 4
 
 
 def dot(left, right):
@@ -59,6 +60,11 @@
         self.tiles = (self.pairs + 1) // 2
         self.message = self.tiles * LANES + 8
         self.cut = model // rows
+        self.first = units // LANES * FIRST // 8 * LANES
+        self.step = TILE if self.first % TILE == 0 and units % TILE == 0 else LANES
+        self.wide = 2 * units - self.first
+        self.narrow = 4 * width
+        self.split = round((self.wide + self.narrow) / (4 * LANES)) * LANES
 
 
 class Place:
@@ -143,6 +149,71 @@
             self.own_copy(k, step, self.p.other()).wait_send()
         for step in range(1, ny):
             self.copy(self.p.group(step), k, ny - 1 + step, self.p.other()).wait_send()
+
+
+class WeightGather:
+    halves = 2
+
+    def __init__(self, place, rows, sems):
+        self.p, self.rows = place, rows
+        self.y_send, self.y_recv, self.x_send, self.x_recv, self.c_send, self.c_recv = sems
+        self.size = place.s.width // (place.s.nx * self.halves)
+
+    def share(self, group, x, half):
+        start = (group * self.p.s.nx + x) * (self.size * self.halves) + half * self.size
+        return self.rows.at[pl.ds(pl.multiple_of(start, self.size), self.size)]
+
+    def slice(self, group):
+        width = self.p.s.width
+        return self.rows.at[pl.ds(pl.multiple_of(group * width, width), width)]
+
+    def y_copy(self, step, half, group):
+        ref = self.share(group, self.p.x, half)
+        at = (step - 1, half)
+        return remote(ref, ref, self.y_send.at[at], self.y_recv.at[at], self.p.along_y(step))
+
+    def x_copy(self, step, side, half, x):
+        ref = self.share(self.p.group(step), x, half)
+        at = (step - 1, side - 1, half)
+        return remote(ref, ref, self.x_send.at[at], self.x_recv.at[at], self.p.along_x(side))
+
+    def c_copy(self, step, group):
+        ref = self.slice(group)
+        return remote(ref, ref, self.c_send.at[step], self.c_recv.at[step], self.p.other())
+
+    def start(self):
+        for half in range(self.halves):
+            for step in range(1, self.p.s.ny):
+                self.y_copy(step, half, self.p.head).start()
+        self.c_copy(0, self.p.head).start()
+
+    def pass_x(self, half):
+        for step in range(1, self.p.s.ny):
+            self.y_copy(step, half, self.p.group(step)).wait_recv()
+            for side in range(1, self.p.s.nx):
+                self.x_copy(step, side, half, self.p.x).start()
+
+    def pass_core(self):
+        nx = self.p.s.nx
+        for step in range(1, self.p.s.ny):
+            for half in range(self.halves):
+                for side in range(1, nx):
+                    self.x_copy(step, side, half, lax.rem(self.p.x + nx - side, nx)).wait_recv()
+            self.c_copy(step, self.p.group(step)).start()
+
+    def finish(self):
+        for step in range(self.p.s.ny):
+            self.c_copy(step, self.p.group(step) + 1 - 2 * self.p.c).wait_recv()
+
+    def sent(self):
+        for step in range(self.p.s.ny):
+            self.c_copy(step, self.p.group(step)).wait_send()
+            if step == 0:
+                continue
+            for half in range(self.halves):
+                self.y_copy(step, half, self.p.head).wait_send()
+                for side in range(1, self.p.s.nx):
+                    self.x_copy(step, side, half, self.p.x).wait_send()
 
 
 class Reduce:
@@ -172,16 +243,20 @@
     def start(self, k):
         self.near_copy(k).start()
 
-    def middle(self, k):
+    def join(self, k):
         self.near_copy(k).wait_recv()
-        for step in range(self.p.s.ny):
-            share = lax.rem(self.p.y + self.p.s.ny - 1 - step, self.p.s.ny)
-            self.near[k, share] = self.near[k, share] + self.parts[k, self.p.c, share]
+        self.near[k] = self.near[k] + self.parts[k, self.p.c]
+
+    def spread(self, k):
         for step in range(1, self.p.s.ny):
             self.far_copy(k, step).start()
 
-    def total(self, k):
-        value = self.near[k, self.p.y]
+    def middle(self, k):
+        self.join(k)
+        self.spread(k)
+
+    def total(self, k, own=None):
+        value = self.near[k, self.p.y] if own is None else own
         for step in range(1, self.p.s.ny):
             self.far_copy(k, step).wait_recv()
             value = value + self.far[step - 1, k]
@@ -193,6 +268,98 @@
     def far_sent(self, k):
         for step in range(1, self.p.s.ny):
             self.far_copy(k, step).wait_send()
+
+
+def flipped(value, mask):
+    bit = 0
+    out = value
+    while mask >> bit:
+        if (mask >> bit) & 1:
+            out = out + (1 - 2 * lax.rem(value // (1 << bit), 2)) * (1 << bit)
+        bit += 1
+    return out
+
+
+def low_zeros(mask, count):
+    return count if mask == 0 else (mask & -mask).bit_length() - 1
+
+
+class Halving:
+    def __init__(self, place, source, near, far, sems, pairs=None, pair_sems=None):
+        self.p, self.source, self.near, self.far = place, source, near, far
+        self.near_send, self.near_recv, self.far_send, self.far_recv = sems
+        self.pairs, self.pair_sems = pairs, pair_sems
+        self.bits = place.s.nz.bit_length() - 1
+        self.first_bit = 0 if pairs is None else 1
+        self.order = list(reversed(range(0, place.s.nz, 1 << self.first_bit)))
+        self.odd = [m for m in reversed(range(place.s.nz)) if m % 2]
+
+    def piece(self, m):
+        return flipped(self.p.z, m)
+
+    def to_z(self, bit):
+        return (flipped(self.p.z, 1 << bit) * self.p.s.nx + self.p.x, self.p.head)
+
+    def at(self, m):
+        return m >> self.first_bit
+
+    def pair_copy(self, m):
+        send, receive = self.pair_sems
+        return remote(
+            self.source(self.piece(m)), self.pairs.at[m >> 1], send.at[m >> 1], receive.at[m >> 1], self.to_z(0)
+        )
+
+    def join_pair(self, m, own):
+        self.pair_copy(m + 1).wait_recv()
+        self.pairs[m >> 1] = self.pairs[m >> 1] + own
+
+    def near_copy(self, m, step):
+        to = lax.rem(self.p.x + step, self.p.s.nx)
+        source = self.source(self.piece(m)) if self.pairs is None else self.pairs.at[m >> 1]
+        at = (step - 1, self.at(m))
+        return remote(
+            source.at[to], self.near.at[at], self.near_send.at[at], self.near_recv.at[at], self.p.along_x(step)
+        )
+
+    def start(self, m):
+        for step in range(1, self.p.s.nx):
+            self.near_copy(m, step).start()
+
+    def join(self, m, own=None):
+        value = self.pairs[m >> 1, self.p.x] if own is None else own
+        for step in range(1, self.p.s.nx):
+            self.near_copy(m, step).wait_recv()
+            value = value + self.near[step - 1, self.at(m)]
+        self.near[0, self.at(m)] = value
+
+    def far_copy(self, m, bit):
+        nz = self.p.s.nz
+        slot = (nz >> self.first_bit) - (nz >> bit) + (m >> (bit + 1))
+        return slot, remote(
+            self.near.at[0, self.at(m)], self.far.at[slot], self.far_send.at[slot], self.far_recv.at[slot], self.to_z(bit)
+        )
+
+    def settle(self, m):
+        for bit in range(self.first_bit, self.bits):
+            slot, copy = self.far_copy(m, bit)
+            if (m >> bit) & 1:
+                copy.start()
+                return
+            copy.wait_recv()
+            self.near[0, self.at(m)] = self.near[0, self.at(m)] + self.far[slot]
+
+    def total(self):
+        return self.near[0, 0]
+
+    def sent(self):
+        if self.pairs is not None:
+            for m in self.odd:
+                self.pair_copy(m).wait_send()
+        for m in self.order:
+            for step in range(1, self.p.s.nx):
+                self.near_copy(m, step).wait_send()
+            if m:
+                self.far_copy(m, low_zeros(m, self.bits))[1].wait_send()
 
 
 def iota(shape, axis):
@@ -283,15 +450,22 @@
         copy.wait()
 
 
+def spread_labels(s, crop_ids, labels_across, labels_down):
+    for k in range(s.chunks):
+        labels = crop_ids[k].astype(WIDE)
+        labels_across[k] = labels
+        labels_down[k * s.chunk : (k + 1) * s.chunk, :] = jnp.broadcast_to(labels, (LANES, s.chunk)).T
+
+
 def block_mask(s, labels_down, labels_across, i, j, turned):
     shape = (s.chunk, s.chunk)
     down, across = iota(shape, 0), iota(shape, 1)
     if turned:
         ordered = (i * s.chunk + across) >= (j * s.chunk + down)
-        equal = labels_down[chunk_rows(s, j), :] == labels_across[i]
+        equal = labels_down[chunk_rows(s, j), 0:1] == labels_across[i]
     else:
         ordered = (i * s.chunk + down) >= (j * s.chunk + across)
-        equal = labels_down[chunk_rows(s, i), :] == labels_across[j]
+        equal = labels_down[chunk_rows(s, i), 0:1] == labels_across[j]
     return jnp.where(ordered & equal, 1.0, 0.0)
 
 
@@ -302,17 +476,33 @@
 def forward_kernel(
     s,
     pixels,
-    labels_down,
-    labels_across,
+    crop_ids,
     first_gain,
     query_weight,
     key_weight,
     value_weight,
     out_weight,
     second_gain,
-    up_weight,
-    down_weight,
-    cotangent,
+    up_source,
+    down_source,
+    cotangent_source,
+    hidden_low,
+    hidden_share,
+    gradient_share,
+    pixel_share,
+    gain_part,
+    prefix_low,
+    latest,
+    near_two,
+    first_out,
+    normed_out,
+    query_out,
+    key_out,
+    values_out,
+    attended_out,
+    denominator_out,
+    key_sum_out,
+    wide_gradient,
     normed,
     query_feature,
     key_feature,
@@ -320,23 +510,19 @@
     attended,
     denominator,
     key_sum,
-    hidden_low,
-    hidden_share,
-    gradient_share,
-    pixel_share,
-    gain_part,
-    prefix_low,
-    latest,
-    middle,
-    wide_gradient,
+    up_weight,
+    down_weight,
+    cotangent,
+    labels_across,
+    labels_down,
     gathered,
-    weight_wide,
+    wide_rows,
     weight_full,
     joined,
     hidden,
     normed_again,
     upward_low,
-    low_wide,
+    middle,
     parts,
     near,
     far,
@@ -345,8 +531,18 @@
     total,
     ones,
     staging,
-    weight_send,
-    weight_recv,
+    first_gradient,
+    first_near,
+    first_far,
+    load_sem,
+    save_sem,
+    staging_sem,
+    weight_y_send,
+    weight_y_recv,
+    weight_x_send,
+    weight_x_recv,
+    weight_c_send,
+    weight_c_recv,
     att_send,
     att_recv,
     low_send,
@@ -357,14 +553,45 @@
     near_recv,
     far_send,
     far_recv,
-    staging_sem,
+    two_send,
+    two_recv,
+    first_near_send,
+    first_near_recv,
+    first_far_send,
+    first_far_recv,
 ):
     p = Place(s)
-    weight_wide[p.head, 0] = out_weight[...].astype(WIDE)
+    loads = [
+        pltpu.make_async_copy(source, target, load_sem.at[i])
+        for i, (source, target) in enumerate(
+            ((up_source, up_weight), (down_source, down_weight), (cotangent_source, cotangent))
+        )
+    ]
+    saves = [
+        pltpu.make_async_copy(source, target, save_sem.at[i])
+        for i, (source, target) in enumerate(
+            (
+                (normed, normed_out),
+                (query_feature, query_out),
+                (key_feature, key_out),
+                (values, values_out),
+                (attended, attended_out),
+                (denominator, denominator_out),
+                (key_sum, key_sum_out),
+            )
+        )
+    ]
+    own_rows = pl.ds(pl.multiple_of(p.head * s.width, s.width), s.width)
+    wide_rows[own_rows, :] = out_weight[...].astype(WIDE)
     p.meet()
-    weights = Gather(p, lambda g, k: weight_wide.at[g, k], weight_send, weight_recv)
-    weights.start(0)
-
+    weights = WeightGather(
+        p, wide_rows, (weight_y_send, weight_y_recv, weight_x_send, weight_x_recv, weight_c_send, weight_c_recv)
+    )
+    weights.start()
+    for load in loads:
+        load.start()
+
+    spread_labels(s, crop_ids, labels_across, labels_down)
     last = labels_across[s.chunks - 1][:, s.chunk - 1 : s.chunk]
     state[...] = jnp.zeros_like(state)
     total[...] = jnp.zeros_like(total)
@@ -380,13 +607,16 @@
             raw = dot(low, weight[...])
             out[at, :] = jnp.where(raw > 0, raw + 1.0, jnp.exp(jnp.minimum(raw, 0.0))).astype(LOW)
         values[at, :] = dot(low, value_weight[...]).astype(LOW)
-        ending = (labels_down[at, :] == last).astype(WIDE)
+        ending = (labels_down[at, 0:1] == last).astype(WIDE)
         kept = key_feature[at, :].astype(WIDE) * ending
         state[...] += dot_left(kept.astype(LOW), values[at, :])
         total[0:1, :] += jnp.sum(kept, axis=0, keepdims=True)
 
     write_message(s, messages.at[0], state, total[0:1, :], last)
     send_messages(p, messages, message_send, message_recv)
+    for save in saves[:4]:
+        save.start()
+    weights.pass_x(0)
 
     @pl.loop(0, s.chunks)
     def _(i):
@@ -408,6 +638,7 @@
 
         lax.fori_loop(0, i + 1, over, 0)
 
+    weights.pass_x(1)
     take_messages(p, messages, message_send, message_recv)
     prefix_total, label = join_messages(p, messages, prefix_low, 1, p.row > 0, True)
     latest[...] = jnp.broadcast_to(label, latest.shape)
@@ -417,7 +648,7 @@
     @pl.loop(0, s.chunks)
     def _(i):
         at = chunk_rows(s, i)
-        matching = (labels_down[at, :] == latest[0:1, 0:1]).astype(WIDE)
+        matching = (labels_down[at, 0:1] == latest[0:1, 0:1]).astype(WIDE)
         query = query_feature[at, :].astype(WIDE)
         numerator = attended[at, :] + dot((query * matching).astype(LOW), prefix_low[...])
         sums = key_sum[at, :] + matching * prefix_total
@@ -429,23 +660,41 @@
         gathered[p.head, i] = value.astype(LOW).astype(WIDE)
         attention.start(i)
 
-    weights.forward(0)
+    for save in saves[4:]:
+        save.start()
+    weights.pass_core()
+    weights.finish()
+    for group in range(s.heads):
+        rows = slice(group * s.width, (group + 1) * s.width)
+        weight_full[rows, :] = wide_rows[rows, :].astype(LOW)
+    weights.sent()
     attention.forward(0)
-    weights.finish(0)
-    weights.sent(0)
-    for group in range(s.heads):
-        weight_full[group * s.width : (group + 1) * s.width, :] = weight_wide[group, 0].astype(LOW)
-
-    hidden_gather = Gather(p, lambda g, k: low_wide.at[k, lax.rem(g, 2), g // 2], low_send, low_recv)
+    for load in loads:
+        load.wait()
+
+    def low_rows(g, k):
+        start = k * s.chunk + (lax.rem(g, 2) * s.ny + g // 2) * s.sub
+        return pl.ds(pl.multiple_of(start, s.sub), s.sub)
+
+    hidden_gather = Gather(p, lambda g, k: wide_rows.at[low_rows(g, k)], low_send, low_recv)
     reduced = Reduce(p, parts, near, far, (near_send, near_recv, far_send, far_recv))
+    two = Reduce(p, parts, near_two, None, (two_send, two_recv, None, None))
+    first = Halving(
+        p,
+        lambda piece: first_gradient.at[piece],
+        first_near,
+        first_far,
+        (first_near_send, first_near_recv, first_far_send, first_far_recv),
+    )
+    order = first.order
     gain_part[...] = jnp.zeros_like(gain_part)
+    shares = (2, s.ny, s.sub, TILE)
 
     def feed_forward(k):
         at = chunk_rows(s, k)
         attention.finish(k)
         for group in range(s.heads):
             joined[:, group * s.width : (group + 1) * s.width] = gathered[group, k].astype(LOW)
-        shares = (2, s.ny, s.sub, TILE)
         for tile in range(s.model // TILE):
             cols = slice(tile * TILE, (tile + 1) * TILE)
             product = dot(joined[...], weight_full[:, cols])
@@ -484,125 +733,112 @@
         part = normalise_back(unit, scale, second_gain[...], grad)
         value = cotangent[k, p.c, p.y].astype(WIDE) + part
         gradient_share[k] = value
-        low_wide[k, p.c, p.y] = value.astype(LOW).astype(WIDE)
+        wide_rows[low_rows(p.head, k), :] = value.astype(LOW).astype(WIDE)
         hidden_gather.start(k)
 
-    def staged(piece, job):
-        return pltpu.make_async_copy(staging.at[job], wide_gradient.at[job, piece], staging_sem.at[job])
-
-    def outer(job, left, right):
-        for piece in range(s.nz):
-            block = left(slice(piece * s.model // s.nz, (piece + 1) * s.model // s.nz))
-            if piece > 0:
-                staged(piece - 1, job).wait()
-            for tile in range(s.units // TILE):
-                cols = slice(tile * TILE, (tile + 1) * TILE)
-                staging[job, :, :, cols] = dot_left(block, right[:, cols]).reshape(s.nx, s.cut, TILE)
-            staged(piece, job).start()
-
-    @pl.loop(0, s.chunks + 3)
+    span = s.nx * s.cut
+
+    def span_of(turn):
+        return pl.ds(pl.multiple_of(first.piece(order[turn]) * span, span), span)
+
+    def first_outer(turn):
+        block = normed_again[:, span_of(turn)]
+        target = first_gradient.at[first.piece(order[turn])]
+        for at in range(0, s.first, s.step):
+            cols = slice(at, at + s.step)
+            target[:, :, cols] = dot_left(block, upward_low[:, cols]).reshape(s.nx, s.cut, s.step)
+        first.start(order[turn])
+
+    def first_join(turn):
+        first.join(order[turn], first_gradient[first.piece(order[turn]), p.x])
+        if order[turn] % 2:
+            first.settle(order[turn])
+
+    def staged(turn):
+        slot = turn % 2
+        return pltpu.make_async_copy(staging.at[slot], wide_gradient.at[first.piece(order[turn])], staging_sem.at[slot])
+
+    def rest_outer(turn):
+        if turn >= 2:
+            staged(turn - 2).wait()
+        target = staging.at[turn % 2]
+        block = normed_again[:, span_of(turn)]
+        for at in range(s.first, s.units, s.step):
+            cols = slice(at - s.first, at - s.first + s.step)
+            value = dot_left(block, upward_low[:, at : at + s.step])
+            target[:, :, cols] = value.reshape(s.nx, s.cut, s.step)
+        block = cotangent[:, :, :, :, span_of(turn)].reshape(s.tokens, span)
+        for at in range(0, s.units, TILE):
+            cols = slice(s.units - s.first + at, s.units - s.first + at + TILE)
+            value = dot_left(block, middle[:, at : at + TILE])
+            target[:, :, cols] = value.reshape(s.nx, s.cut, TILE)
+        staged(turn).start()
+
+    @pl.loop(0, s.chunks)
     def _(k):
-        @pl.when(k < s.chunks)
-        def _():
-            feed_forward(k)
-
-        @pl.when((k >= 1) & (k <= s.chunks))
+        feed_forward(k)
+
+        @pl.when(k >= 1)
         def _():
             reduced.middle(k - 1)
 
-        @pl.when(k == s.chunks)
-        def _():
-            outer(0, lambda cols: normed_again[:, cols], upward_low)
-
-        @pl.when((k >= 2) & (k <= s.chunks + 1))
-        def _():
-            second_norm_back(k - 2)
-
-        @pl.when(k == s.chunks + 1)
-        def _():
-            outer(1, lambda cols: cotangent_rows(s, cotangent, cols), middle)
-
-        @pl.when((k >= 3) & (k <= s.chunks + 2))
-        def _():
-            hidden_gather.forward(k - 3)
-
+    end = s.chunks
+    first_outer(0)
+    reduced.middle(end - 1)
+    for turn in range(1, s.nz):
+        first_outer(turn)
+    for k in range(end - 2):
+        second_norm_back(k)
+    rest_outer(0)
+    for k in range(end - 2, end):
+        second_norm_back(k)
+        first_join(k - end + 2)
+        rest_outer(k - end + 3)
+    for turn in range(3, s.nz):
+        rest_outer(turn)
+
+    @pl.loop(0, s.chunks)
+    def _(k):
+        reduced.near_sent(k)
+        low = middle[chunk_rows(s, k), :]
+        for tile in range(s.model // TILE):
+            cols = slice(tile * TILE, (tile + 1) * TILE)
+            parts[k, :, :, :, cols] = dot(low, down_weight[:, cols]).reshape(shares)
+        two.start(k)
+
+    for turn in range(2, s.nz):
+        first_join(turn)
+        if order[turn] % 2:
+            first.settle(order[turn] + 1)
     for k in range(s.chunks):
+        two.join(k)
         pixel_share[k] = pixels[k, p.c, p.y]
+    for k in range(end - 2):
+        hidden_gather.forward(k)
+    first.settle(0)
+    for k in range(end - 2, end):
+        hidden_gather.forward(k)
+
+    for k in range(s.chunks):
         hidden_gather.finish(k)
-        hidden_low[k * s.chunk : (k + 1) * s.chunk, :] = low_wide[k].reshape(s.chunk, s.model).astype(LOW)
-    for job in range(2):
-        staged(s.nz - 1, job).wait()
+        rows = slice(k * s.chunk, (k + 1) * s.chunk)
+        hidden_low[rows, :] = wide_rows[rows, :].astype(LOW)
+    first_out[...] = first.total()
+    first.sent()
+    for turn in range(max(0, s.nz - 2), s.nz):
+        staged(turn).wait()
     for k in range(s.chunks):
         attention.sent(k)
         hidden_gather.sent(k)
-        reduced.near_sent(k)
         reduced.far_sent(k)
-
-
-def cotangent_rows(s, cotangent, cols):
-    return cotangent[:, :, :, :, cols].reshape(s.tokens, cols.stop - cols.start)
-
-
-class Scatter:
-    def __init__(self, place, source, near, far, sems):
-        self.p, self.source, self.near, self.far = place, source, near, far
-        self.near_send, self.near_recv, self.far_send, self.far_recv = sems
-
-    def piece(self, turn):
-        return lax.rem(self.p.z + turn + 1, self.p.s.nz)
-
-    def near_copy(self, turn, step):
-        to = lax.rem(self.p.x + step, self.p.s.nx)
-        return remote(
-            self.source.at[self.piece(turn), to],
-            self.near.at[step - 1, turn],
-            self.near_send.at[step - 1, turn],
-            self.near_recv.at[step - 1, turn],
-            self.p.along_x(step),
-        )
-
-    def far_copy(self, turn):
-        return remote(
-            self.near.at[0, turn],
-            self.far.at[turn],
-            self.far_send.at[turn],
-            self.far_recv.at[turn],
-            self.p.along_z(turn + 1),
-        )
-
-    def start(self, turn):
-        for step in range(1, self.p.s.nx):
-            self.near_copy(turn, step).start()
-
-    def middle(self, turn, own):
-        value = own
-        for step in range(1, self.p.s.nx):
-            self.near_copy(turn, step).wait_recv()
-            value = value + self.near[step - 1, turn]
-        self.near[0, turn] = value
-        if turn < self.p.s.nz - 1:
-            self.far_copy(turn).start()
-
-    def total(self):
-        value = self.near[0, self.p.s.nz - 1]
-        for turn in range(self.p.s.nz - 1):
-            self.far_copy(turn).wait_recv()
-            value = value + self.far[turn]
-        return value
-
-    def sent(self):
-        for turn in range(self.p.s.nz):
-            for step in range(1, self.p.s.nx):
-                self.near_copy(turn, step).wait_send()
-        for turn in range(self.p.s.nz - 1):
-            self.far_copy(turn).wait_send()
+        two.near_sent(k)
+    for save in saves:
+        save.wait()
 
 
 def backward_kernel(
     s,
-    labels_down,
-    labels_across,
-    normed,
+    crop_ids,
     query_feature,
     key_feature,
     values,
@@ -610,34 +846,39 @@
     denominator,
     key_sum,
     hidden_low,
-    hidden_share,
-    gradient_share,
-    pixel_share,
     gain_part,
     prefix_low,
     latest,
-    middle,
-    down_weight,
     query_weight,
     key_weight,
     value_weight,
     out_weight,
     first_gain,
+    near_two,
+    normed_source,
+    hidden_source,
+    gradient_source,
+    pixel_source,
     wide_gradient,
-    result,
     gains,
-    up_out,
-    down_out,
+    wide_out,
     narrow_out,
-    pixel_gradient,
-    result_wide,
+    pixel_out,
+    result_out,
+    normed,
+    hidden_share,
+    gradient_share,
+    pixel_share,
+    two_own,
+    labels_across,
+    labels_down,
     parts,
-    near_two,
     far_two,
     near_four,
     far_four,
-    result_own,
-    pixel_own,
+    result_wide,
+    result_low,
+    pixel_gradient,
     numerator_low,
     denominator_back,
     spread_back,
@@ -652,19 +893,20 @@
     messages,
     narrow_gradient,
     own_wide,
-    near_up,
-    far_up,
-    near_down,
-    far_down,
+    own_pairs,
+    near_wide,
+    far_wide,
+    near_split,
+    far_split,
+    pairs_split,
     near_narrow,
     far_narrow,
     gain_heads,
     gain_x,
     gain_z,
+    load_sem,
     message_send,
     message_recv,
-    two_near_send,
-    two_near_recv,
     two_far_send,
     two_far_recv,
     four_near_send,
@@ -675,79 +917,128 @@
     result_recv,
     pixel_send,
     pixel_recv,
-    scatter_near_send,
-    scatter_near_recv,
-    scatter_far_send,
-    scatter_far_recv,
+    wide_near_send,
+    wide_near_recv,
+    wide_far_send,
+    wide_far_recv,
+    split_near_send,
+    split_near_recv,
+    split_far_send,
+    split_far_recv,
+    split_send,
+    split_recv,
+    narrow_near_send,
+    narrow_near_recv,
+    narrow_far_send,
+    narrow_far_recv,
     gain_send,
     gain_recv,
     own_sem,
+    pairs_sem,
     result_sem,
     pixel_sem,
-    read_sem,
 ):
     p = Place(s)
     p.meet()
-
-    def scatter(job, source, near, far):
-        sems = (
-            scatter_near_send.at[job],
-            scatter_near_recv.at[job],
-            scatter_far_send.at[job],
-            scatter_far_recv.at[job],
+    two = Reduce(p, None, near_two, far_two, (None, None, two_far_send, two_far_recv))
+    four = Reduce(p, parts, near_four, far_four, (four_near_send, four_near_recv, four_far_send, four_far_recv))
+    wide = Halving(
+        p,
+        lambda piece: wide_gradient.at[piece, :, :, s.split :],
+        near_wide,
+        far_wide,
+        (wide_near_send, wide_near_recv, wide_far_send, wide_far_recv),
+    )
+    split = Halving(
+        p,
+        lambda piece: wide_gradient.at[piece, :, :, 0 : s.split],
+        near_split,
+        far_split,
+        (split_near_send, split_near_recv, split_far_send, split_far_recv),
+        pairs_split,
+        (split_send, split_recv),
+    )
+    sides = (slice(0, s.narrow // 2), slice(s.narrow // 2, s.narrow))
+
+    def narrow_job(i):
+        sems = (narrow_near_send.at[i], narrow_near_recv.at[i], narrow_far_send.at[i], narrow_far_recv.at[i])
+        return Halving(
+            p, lambda piece: narrow_gradient.at[piece, :, :, sides[i]], near_narrow.at[i], far_narrow.at[i], sems
         )
-        return Scatter(p, source, near, far, sems)
-
-    up = scatter(0, wide_gradient.at[0], near_up, far_up)
-    down = scatter(1, wide_gradient.at[1], near_down, far_down)
-    narrow = scatter(2, narrow_gradient, near_narrow, far_narrow)
-    jobs = (up, down, narrow)
-    wide = 2 * s.nz
-    flight = {"next": 0, "ready": wide}
+
+    narrow = (narrow_job(0), narrow_job(1))
+    jobs = (wide, split) + narrow
+    steps = [(job, m) for job in jobs for m in job.order]
+    flight = {"next": 0, "ready": s.nz, "taken": 0}
+    pending = []
+
+    def settle_ready(at):
+        for entry in list(pending):
+            if entry[0] <= at:
+                entry[1].settle(entry[2])
+                pending.remove(entry)
 
     def push(limit):
         while flight["next"] <= limit and flight["next"] < flight["ready"]:
-            at = flight["next"]
-            jobs[at // s.nz].start(at % s.nz)
-            flight["next"] = at + 1
-
-    def own_load(at):
-        job, turn = at // s.nz, at % s.nz
-        source = wide_gradient.at[job, jobs[job].piece(turn), p.x]
-        return pltpu.make_async_copy(source, own_wide.at[at % 2], own_sem.at[at % 2])
-
-    def take(at):
-        job, turn = at // s.nz, at % s.nz
-        if at < wide:
+            job, m = steps[flight["next"]]
+            job.start(m)
+            flight["next"] += 1
+
+    def own_load(turn):
+        source = wide_gradient.at[wide.piece(wide.order[turn]), p.x, :, s.split :]
+        return pltpu.make_async_copy(source, own_wide.at[turn % 2], own_sem.at[turn % 2])
+
+    def pairs_load(m):
+        source = wide_gradient.at[split.piece(m), :, :, 0 : s.split]
+        return pltpu.make_async_copy(source, own_pairs.at[m >> 1], pairs_sem.at[m >> 1])
+
+    def take():
+        at = flight["taken"]
+        flight["taken"] = at + 1
+        job, m = steps[at]
+        if job is wide:
             own_load(at).wait()
-            jobs[job].middle(turn, own_wide[at % 2])
+            wide.join(m, own_wide[at % 2])
+            if at + 2 < s.nz:
+                own_load(at + 2).start()
+        elif job is split:
+            split.join(m)
         else:
-            narrow.middle(turn, narrow_gradient[narrow.piece(turn), p.x])
-        if at + 2 < wide:
-            own_load(at + 2).start()
+            job.join(m, narrow_gradient[job.piece(m), p.x, :, sides[narrow.index(job)]])
         push(at + AHEAD)
-
+        if (m >> job.first_bit) & 1:
+            job.settle(m)
+        else:
+            pending.append((at + 1 if m else at + 2, job, m))
+        settle_ready(at)
+
+    for m in split.odd:
+        split.pair_copy(m).start()
     push(0)
+    for k in range(s.chunks):
+        two.spread(k)
+    loads = [
+        pltpu.make_async_copy(source, target, load_sem.at[i])
+        for i, (source, target) in enumerate(
+            (
+                (near_two.at[:, p.y], two_own),
+                (hidden_source, hidden_share),
+                (gradient_source, gradient_share),
+                (pixel_source, pixel_share),
+                (normed_source, normed),
+            )
+        )
+    ]
+    for load in loads:
+        load.start()
     own_load(0).start()
     own_load(1).start()
-    two = Reduce(p, parts, near_two, far_two, (two_near_send, two_near_recv, two_far_send, two_far_recv))
-    four = Reduce(p, parts, near_four, far_four, (four_near_send, four_near_recv, four_far_send, four_far_recv))
-    result_gather = Gather(
-        p,
-        lambda g, k: result_wide.at[k, lax.rem(g, 2), g // 2],
-        result_send,
-        result_recv,
-        lambda k: result_own.at[k],
-    )
-    pixel_gather = Gather(
-        p,
-        lambda g, k: pixel_gradient.at[k, lax.rem(g, 2), g // 2],
-        pixel_send,
-        pixel_recv,
-        lambda k: pixel_own.at[k],
-    )
+    for m in split.order:
+        pairs_load(m).start()
+    result_gather = Gather(p, lambda g, k: result_wide.at[k, lax.rem(g, 2), g // 2], result_send, result_recv)
+    pixel_gather = Gather(p, lambda g, k: pixel_gradient.at[k, lax.rem(g, 2), g // 2], pixel_send, pixel_recv)
     shares = (2, s.ny, s.sub, TILE)
-
+    spread_labels(s, crop_ids, labels_across, labels_down)
     first = labels_across[0][:, 0:1]
     state[...] = jnp.zeros_like(state)
     total[...] = jnp.zeros_like(total)
@@ -765,27 +1056,13 @@
         query = query_feature[at, :].astype(WIDE)
         spread = slope * query
         spread_back[at, :] = spread.astype(LOW)
-        leading = (labels_down[at, :] == first).astype(WIDE)
+        leading = (labels_down[at, 0:1] == first).astype(WIDE)
         state[...] += dot_left((query * leading).astype(LOW), low)
         total[0:1, :] += jnp.sum(spread * leading, axis=0, keepdims=True)
 
     write_message(s, messages.at[0], state, total[0:1, :], first)
     send_messages(p, messages, message_send, message_recv)
     push(AHEAD - 1)
-
-    @pl.loop(0, s.chunks)
-    def _(k):
-        low = middle[chunk_rows(s, k), :]
-        for tile in range(s.model // TILE):
-            cols = slice(tile * TILE, (tile + 1) * TILE)
-            parts[k, :, :, :, cols] = dot(low, down_weight[:, cols]).reshape(shares)
-        two.start(k)
-
-    @pl.loop(0, s.chunks)
-    def _(k):
-        two.middle(k)
-
-    take(0)
 
     @pl.loop(0, s.chunks)
     def _(i):
@@ -805,7 +1082,7 @@
 
         lax.fori_loop(0, i + 1, over, 0)
 
-    take(1)
+    take()
 
     @pl.loop(0, s.chunks)
     def _(j):
@@ -830,20 +1107,27 @@
 
         lax.fori_loop(j, s.chunks, over, 0)
 
+    for load in loads:
+        load.wait()
+    take()
+
     @pl.loop(0, s.chunks)
     def _(k):
-        result_own[k] = (hidden_share[k] + two.total(k)).astype(LOW).astype(WIDE)
-        result_gather.start(k)
+        value = hidden_share[k] + two.total(k, two_own[k])
+        result_wide[k, p.c, p.y] = value.astype(LOW).astype(WIDE)
+
+        @pl.when(k < s.chunks // 2)
+        def _():
+            result_gather.start(k)
 
     take_messages(p, messages, message_send, message_recv)
-    suffix_total, label = join_messages(p, messages, suffix_low, s.rows - 1, p.row < s.rows - 1, False)
-    following = label
+    suffix_total, following = join_messages(p, messages, suffix_low, s.rows - 1, p.row < s.rows - 1, False)
 
     @pl.loop(0, s.chunks)
     def _(k):
         at = chunk_rows(s, k)
-        matching = (labels_down[at, :] == latest[0:1, 0:1]).astype(WIDE)
-        later = (labels_down[at, :] == following).astype(WIDE)
+        matching = (labels_down[at, 0:1] == latest[0:1, 0:1]).astype(WIDE)
+        later = (labels_down[at, 0:1] == following).astype(WIDE)
         query, key = query_feature[at, :], key_feature[at, :]
         value = query_back[at, :] + matching * dot_right(numerator_low[at, :], prefix_low[...])
         low = (value * jnp.minimum(query.astype(WIDE), 1.0)).astype(LOW)
@@ -854,7 +1138,6 @@
         narrow_low[0, at, :] = low
         narrow_low[1, at, :] = key_low
         narrow_low[2, at, :] = value_low
-        two.near_sent(k)
         for tile in range(s.model // TILE):
             cols = slice(tile * TILE, (tile + 1) * TILE)
             product = (
@@ -865,12 +1148,16 @@
             parts[k, :, :, :, cols] = product.reshape(shares)
         four.start(k)
 
-
     @pl.loop(0, s.chunks)
     def _(k):
         four.middle(k)
 
-    take(2)
+    take()
+    for m in split.order:
+        pairs_load(m).wait()
+        split.join_pair(m, own_pairs[m >> 1])
+    flight["ready"] = len(wide.order) + len(split.order)
+
     span = s.nx * s.cut
     for piece in range(s.nz):
         cols = slice(piece * span, (piece + 1) * span)
@@ -880,38 +1167,35 @@
         for part in range(3):
             product = dot_left(normed[:, cols], narrow_low[part])
             narrow_gradient[piece, :, :, (part + 1) * s.width : (part + 2) * s.width] = product.reshape(shape)
-    flight["ready"] = 3 * s.nz
-    rest = list(range(3, 3 * s.nz))
-
-    def take_some(count):
-        for at in rest[:count]:
-            take(at)
-        del rest[:count]
+    flight["ready"] = len(steps)
 
     def take_until_left(count):
-        take_some(max(0, len(rest) - count))
-
-    take_until_left(7)
-    gain_heads[0] = gain_part[...]
-
-    def result_local(k):
-        return pltpu.make_async_copy(result_own.at[k], result_wide.at[k, p.c, p.y], result_sem.at[k])
-
-    def pixel_local(k):
-        return pltpu.make_async_copy(pixel_own.at[k], pixel_gradient.at[k, p.c, p.y], pixel_sem.at[k])
-
-    def result_read(k):
-        return pltpu.make_async_copy(result_wide.at[k], parts.at[k], read_sem.at[k])
-
-    @pl.loop(0, s.chunks)
-    def _(k):
+        while len(steps) - flight["taken"] > count:
+            take()
+
+    left = 2 * s.nz
+    take_until_left(left + len(split.order))
+    gain_x[0] = gain_part[...]
+
+    def result_copy(k):
+        rows = pl.ds(k * s.chunk, s.chunk)
+        return pltpu.make_async_copy(result_low.at[rows], result_out.at[rows], result_sem.at[k])
+
+    def pixel_copy(k):
+        return pltpu.make_async_copy(pixel_gradient.at[k], pixel_out.at[k], pixel_sem.at[k])
+
+    def first_norm_back(k):
         grad = four.total(k)
         unit, scale = normalise(pixel_share[k].astype(WIDE))
-        gain_heads[0, 1:2, :] += jnp.sum(grad * unit, axis=0, keepdims=True)
-        pixel_own[k] = gradient_share[k] + normalise_back(unit, scale, first_gain[...], grad)
+        gain_x[0, 1:2, :] += jnp.sum(grad * unit, axis=0, keepdims=True)
+        pixel_gradient[k, p.c, p.y] = gradient_share[k] + normalise_back(unit, scale, first_gain[...], grad)
         pixel_gather.start(k)
-        pixel_local(k).start()
-        result_local(k).start()
+
+    for k in range(s.chunks // 2):
+        first_norm_back(k)
+    take_until_left(left + len(split.order) // 2)
+    for k in range(s.chunks // 2, s.chunks):
+        first_norm_back(k)
 
     def gain_copies(index, buffer, device):
         return [
@@ -932,46 +1216,114 @@
         return value
 
     rounds = (
-        (0, gain_heads, p.along_heads),
-        (1, gain_x, p.along_x),
-        (2, gain_z, p.along_z),
+        (0, gain_x, p.along_x),
+        (1, gain_z, p.along_z),
+        (2, gain_heads, p.along_heads),
     )
     gain_start(*rounds[0])
-    take_until_left(5)
+    for k in range(s.chunks // 2, s.chunks):
+        result_gather.start(k)
+    take_until_left(left)
+    for k in range(s.chunks // 2):
+        result_gather.forward(k)
+    take_until_left(left - 2)
+    gain_z[0] = gain_total(*rounds[0])
+    gain_start(*rounds[1])
+    for k in range(s.chunks // 2):
+        pixel_gather.forward(k)
+    take_until_left(left - 4)
+    gain_heads[0] = gain_total(*rounds[1])
+    gain_start(*rounds[2])
+    for k in range(s.chunks // 2, s.chunks):
+        pixel_gather.forward(k)
+    for k in range(s.chunks // 2, s.chunks):
+        result_gather.forward(k)
+    take_until_left(2)
     for k in range(s.chunks):
-        result_gather.forward(k)
-    gain_x[0] = gain_total(*rounds[0])
-    gain_start(*rounds[1])
-    take_until_left(4)
-    for k in range(s.chunks):
-        pixel_gather.forward(k)
-    take_until_left(3)
-    gain_z[0] = gain_total(*rounds[1])
-    gain_start(*rounds[2])
+        pixel_gather.finish(k)
+        pixel_copy(k).start()
     for k in range(s.chunks):
         result_gather.finish(k)
-        result_local(k).wait()
-        four.near_sent(k)
-        result_read(k).start()
+        result_low[k * s.chunk : (k + 1) * s.chunk, :] = result_wide[k].reshape(s.chunk, s.model).astype(LOW)
+        result_copy(k).start()
+    gains[...] = gain_total(*rounds[2])
+    take_until_left(0)
+    wide_out[:, s.split :] = wide.total()
+    wide_out[:, 0 : s.split] = split.total()
+    settle_ready(len(steps) + 2)
+    for job, side in zip(narrow, sides):
+        narrow_out[:, side] = job.total()
     for k in range(s.chunks):
-        result_read(k).wait()
-        result[k * s.chunk : (k + 1) * s.chunk, :] = parts[k].reshape(s.chunk, s.model).astype(LOW)
-    take_until_left(2)
-    up_out[...] = up.total()
-    gains[...] = gain_total(*rounds[2])
-    take_until_left(1)
-    for k in range(s.chunks):
-        pixel_gather.finish(k)
-        pixel_local(k).wait()
+        result_copy(k).wait()
+        pixel_copy(k).wait()
         pixel_gather.sent(k)
         result_gather.sent(k)
         two.far_sent(k)
+        four.near_sent(k)
         four.far_sent(k)
-    take_until_left(0)
-    down_out[...] = down.total()
-    narrow_out[...] = narrow.total()
     for job in jobs:
         job.sent()
+
+
+def finish_kernel(
+    s,
+    first_out,
+    wide_out,
+    narrow_out,
+    gains,
+    pixel_source,
+    result_source,
+    up_gradient,
+    down_gradient,
+    out_gradient,
+    query_gradient,
+    key_gradient,
+    value_gradient,
+    first_gain,
+    second_gain,
+    pixel_gradient,
+    result,
+    pixel_rows,
+    result_rows,
+    read_sem,
+    write_sem,
+):
+    row = lax.axis_index("rows")
+
+    def places(i, k):
+        rows = pl.ds(k * s.chunk, s.chunk)
+        if i == 0:
+            return pixel_source.at[k], pixel_rows.at[k], pixel_gradient.at[k]
+        return result_source.at[rows], result_rows.at[rows], result.at[rows]
+
+    def read(i, k):
+        source, between, unused = places(i, k)
+        return pltpu.make_async_copy(source, between, read_sem.at[i, k])
+
+    def write(i, k):
+        unused, between, target = places(i, k)
+        return pltpu.make_async_copy(between, target, write_sem.at[i, k])
+
+    moves = [(i, k) for k in range(s.chunks) for i in range(2)]
+    for move in moves:
+        read(*move).start()
+    rest = s.units - s.first
+    up_gradient[:, 0 : s.first] = first_out[...]
+    up_gradient[:, s.first :] = wide_out[:, 0:rest]
+    down_gradient[...] = wide_out[:, rest:].T
+    out_gradient[...] = narrow_out[:, 0 : s.width].T
+    for i, target in enumerate((query_gradient, key_gradient, value_gradient)):
+        target[...] = narrow_out[:, (i + 1) * s.width : (i + 2) * s.width]
+    own = jnp.zeros((8, s.cut), WIDE)
+    for at in range(s.rows):
+        own = own + jnp.where(row == at, gains[:, at * s.cut : (at + 1) * s.cut], 0.0)
+    second_gain[...] = own[0:1]
+    first_gain[...] = own[1:2]
+    for move in moves:
+        read(*move).wait()
+        write(*move).start()
+    for move in moves:
+        write(*move).wait()
 
 
 def vmem(count):
@@ -1001,9 +1353,7 @@
     s = Sizes(rows, heads, tokens, model, query_weight.shape[1], up_weight.shape[1])
     whole = (s.chunks, 2, s.ny, s.sub, model)
     share = (s.chunks, s.sub, model)
-    labels = crop_ids.astype(WIDE)
-    labels_down = labels.reshape(tokens, 1)
-    labels_across = labels.reshape(s.chunks, 1, s.chunk)
+    labels = crop_ids.reshape(s.chunks, 1, s.chunk)
     shape = jax.ShapeDtypeStruct
     any_space = pl.BlockSpec(memory_space=pl.ANY)
 
@@ -1015,17 +1365,34 @@
             dma(s.ny - 1, s.chunks),
         ]
 
-    def gather_sems(count):
-        return [dma(2 * s.ny - 1, count), dma(heads, count)]
-
+    def gather_sems():
+        return [dma(2 * s.ny - 1, s.chunks), dma(heads, s.chunks)]
+
+    def scatter_sems():
+        return [
+            dma(s.nx - 1, s.nz),
+            dma(s.nx - 1, s.nz),
+            dma(s.nz - 1),
+            dma(s.nz - 1),
+        ]
+
+    def scatter_buffers(width, pieces=s.nz):
+        return [
+            pltpu.VMEM((s.nx - 1, pieces, s.cut, width), WIDE),
+            pltpu.VMEM((pieces - 1, s.cut, width), WIDE),
+        ]
+
+    half = s.nz // 2
+
+    lows = [(tokens, model)] + [(tokens, s.width)] * 3
+    wides = [(tokens, s.width)] * 3
+    near = (s.chunks, s.ny, s.sub, model)
+    far = (s.ny - 1,) + share
+    label_buffers = [
+        pltpu.VMEM((s.chunks, 1, s.chunk), WIDE),
+        pltpu.VMEM((tokens, LANES), WIDE),
+    ]
     outs = [
-        shape((tokens, model), LOW),
-        shape((tokens, s.width), LOW),
-        shape((tokens, s.width), LOW),
-        shape((tokens, s.width), LOW),
-        shape((tokens, s.width), WIDE),
-        shape((tokens, s.width), WIDE),
-        shape((tokens, s.width), WIDE),
         shape((tokens, model), LOW),
         shape(share, WIDE),
         shape(share, WIDE),
@@ -1033,10 +1400,23 @@
         shape((8, model), WIDE),
         shape((s.width, s.width), LOW),
         shape((8, LANES), WIDE),
-        shape((tokens, s.units), LOW),
-        shape((2, s.nz, s.nx, s.cut, s.units), WIDE),
+        shape(near, WIDE),
+        shape((s.cut, s.first), WIDE),
+        *[shape(size, LOW) for size in lows],
+        *[shape(size, WIDE) for size in wides],
+        shape((s.nz, s.nx, s.cut, s.wide), WIDE),
     ]
+    shared = WeightGather.halves
     (
+        hidden_low,
+        hidden_share,
+        gradient_share,
+        pixel_share,
+        gain_part,
+        prefix_low,
+        latest,
+        near_two,
+        first_out,
         normed,
         query_feature,
         key_feature,
@@ -1044,44 +1424,51 @@
         attended,
         denominator,
         key_sum,
-        hidden_low,
-        hidden_share,
-        gradient_share,
-        pixel_share,
-        gain_part,
-        prefix_low,
-        latest,
-        middle,
         wide_gradient,
     ) = pl.pallas_call(
         functools.partial(forward_kernel, s),
         out_shape=outs,
-        in_specs=vmem(12),
-        out_specs=vmem(15) + [any_space],
+        in_specs=vmem(8) + [any_space] * 3,
+        out_specs=vmem(9) + [any_space] * 8,
         scratch_shapes=[
+            *[pltpu.VMEM(size, LOW) for size in lows],
+            *[pltpu.VMEM(size, WIDE) for size in wides],
+            pltpu.VMEM((model, s.units), LOW),
+            pltpu.VMEM((s.units, model), LOW),
+            pltpu.VMEM(whole, LOW),
+            *label_buffers,
             pltpu.VMEM((heads, s.chunks, s.chunk, s.width), WIDE),
-            pltpu.VMEM((heads, 1, s.width, model), WIDE),
+            pltpu.VMEM((max(tokens, model), model), WIDE),
             pltpu.VMEM((model, model), LOW),
             pltpu.VMEM((s.chunk, model), LOW),
             pltpu.VMEM(whole[1:], WIDE),
             pltpu.VMEM((tokens, model), LOW),
             pltpu.VMEM((tokens, s.units), LOW),
+            pltpu.VMEM((tokens, s.units), LOW),
             pltpu.VMEM(whole, WIDE),
-            pltpu.VMEM(whole, WIDE),
-            pltpu.VMEM((s.chunks, s.ny, s.sub, model), WIDE),
-            pltpu.VMEM((s.ny - 1,) + share, WIDE),
+            pltpu.VMEM(near, WIDE),
+            pltpu.VMEM(far, WIDE),
             pltpu.VMEM((rows, s.message, LANES), WIDE),
             pltpu.VMEM((s.width, s.width), WIDE),
             pltpu.VMEM((8, s.width), WIDE),
             pltpu.VMEM((s.width, s.width), LOW),
-            pltpu.VMEM((2, s.nx, s.cut, s.units), WIDE),
-            *gather_sems(1),
-            *gather_sems(s.chunks),
-            *gather_sems(s.chunks),
+            pltpu.VMEM((2, s.nx, s.cut, s.wide), WIDE),
+            pltpu.VMEM((s.nz, s.nx, s.cut, s.first), WIDE),
+            *scatter_buffers(s.first),
+            dma(3),
+            dma(7),
+            dma(2),
+            *[dma(s.ny - 1, shared)] * 2,
+            *[dma(s.ny - 1, s.nx - 1, shared)] * 2,
+            *[dma(s.ny)] * 2,
+            *gather_sems(),
+            *gather_sems(),
             dma(rows),
             dma(rows),
             *reduce_sems(),
-            dma(2),
+            dma(s.chunks),
+            dma(s.chunks),
+            *scatter_sems(),
         ],
         compiler_params=pltpu.CompilerParams(
             collective_id=0, has_side_effects=True, vmem_limit_bytes=60 << 20
@@ -1089,8 +1476,7 @@
         name="forward_part",
     )(
         pixels.reshape(whole),
-        labels_down,
-        labels_across,
+        labels,
         first_gain.reshape(1, model),
         query_weight,
         key_weight,
@@ -1101,74 +1487,70 @@
         down_weight,
         cotangent.reshape(whole),
     )
-    columns = 4 * s.width
     outs = [
+        shape((8, model), WIDE),
+        shape((s.cut, s.wide), WIDE),
+        shape((s.cut, s.narrow), WIDE),
+        shape(whole, WIDE),
         shape((tokens, model), LOW),
-        shape((8, model), WIDE),
-        shape((s.cut, s.units), WIDE),
-        shape((s.cut, s.units), WIDE),
-        shape((s.cut, columns), WIDE),
-        shape(whole, WIDE),
-        shape(whole, WIDE),
     ]
-
-    def scatter_buffers(width):
-        return [
-            pltpu.VMEM((s.nx - 1, s.nz, s.cut, width), WIDE),
-            pltpu.VMEM((s.nz - 1, s.cut, width), WIDE),
-        ]
-
-    def reduce_buffers():
-        return [
-            pltpu.VMEM((s.chunks, s.ny, s.sub, model), WIDE),
-            pltpu.VMEM((s.ny - 1,) + share, WIDE),
-        ]
-
-    result, gains, up_out, down_out, narrow_out, pixel_gradient, unused = pl.pallas_call(
+    gains, wide_out, narrow_out, pixel_wide, result_low = pl.pallas_call(
         functools.partial(backward_kernel, s),
         out_shape=outs,
-        in_specs=vmem(23) + [any_space],
-        out_specs=vmem(5) + [any_space] * 2,
+        in_specs=vmem(16) + [any_space] * 6,
+        out_specs=vmem(3) + [any_space] * 2,
         scratch_shapes=[
-            pltpu.VMEM(whole, WIDE),
-            *reduce_buffers(),
-            *reduce_buffers(),
+            pltpu.VMEM((tokens, model), LOW),
             pltpu.VMEM(share, WIDE),
             pltpu.VMEM(share, WIDE),
+            pltpu.VMEM(share, LOW),
+            pltpu.VMEM(share, WIDE),
+            *label_buffers,
+            pltpu.VMEM(whole, WIDE),
+            pltpu.VMEM(far, WIDE),
+            pltpu.VMEM(near, WIDE),
+            pltpu.VMEM(far, WIDE),
+            pltpu.VMEM(whole, WIDE),
+            pltpu.VMEM((tokens, model), LOW),
+            pltpu.VMEM(whole, WIDE),
             pltpu.VMEM((tokens, s.width), LOW),
             pltpu.VMEM((tokens, s.width), WIDE),
             pltpu.VMEM((tokens, s.width), LOW),
-            pltpu.VMEM((tokens, s.width), WIDE),
-            pltpu.VMEM((tokens, s.width), WIDE),
-            pltpu.VMEM((tokens, s.width), WIDE),
+            *[pltpu.VMEM((tokens, s.width), WIDE)] * 3,
             pltpu.VMEM((3, tokens, s.width), LOW),
             pltpu.VMEM((s.width, s.width), LOW),
             pltpu.VMEM((s.width, s.width), WIDE),
             pltpu.VMEM((8, s.width), WIDE),
             pltpu.VMEM((s.width, s.width), LOW),
             pltpu.VMEM((rows, s.message, LANES), WIDE),
-            pltpu.VMEM((s.nz, s.nx, s.cut, columns), WIDE),
-            pltpu.VMEM((2, s.cut, s.units), WIDE),
-            *scatter_buffers(s.units),
-            *scatter_buffers(s.units),
-            *scatter_buffers(columns),
+            pltpu.VMEM((s.nz, s.nx, s.cut, s.narrow), WIDE),
+            pltpu.VMEM((2, s.cut, s.wide - s.split), WIDE),
+            pltpu.VMEM((half, s.nx, s.cut, s.split), WIDE),
+            *scatter_buffers(s.wide - s.split),
+            *scatter_buffers(s.split, half),
+            pltpu.VMEM((half, s.nx, s.cut, s.split), WIDE),
+            pltpu.VMEM((2, s.nx - 1, s.nz, s.cut, s.narrow // 2), WIDE),
+            pltpu.VMEM((2, s.nz - 1, s.cut, s.narrow // 2), WIDE),
             pltpu.VMEM((heads, 8, model), WIDE),
             pltpu.VMEM((s.nx, 8, model), WIDE),
             pltpu.VMEM((s.nz, 8, model), WIDE),
+            dma(5),
             dma(rows),
             dma(rows),
+            *reduce_sems()[2:],
             *reduce_sems(),
-            *reduce_sems(),
-            *gather_sems(s.chunks),
-            *gather_sems(s.chunks),
-            dma(3, s.nx - 1, s.nz),
-            dma(3, s.nx - 1, s.nz),
-            dma(3, s.nz - 1),
-            dma(3, s.nz - 1),
+            *gather_sems(),
+            *gather_sems(),
+            *scatter_sems(),
+            *scatter_sems(),
+            dma(half),
+            dma(half),
+            *[dma(2, s.nx - 1, s.nz)] * 2,
+            *[dma(2, s.nz - 1)] * 2,
             dma(3, max(heads, s.nx, s.nz)),
             dma(3, max(heads, s.nx, s.nz)),
             dma(2),
-            dma(s.chunks),
+            dma(half),
             dma(s.chunks),
             dma(s.chunks),
         ],
@@ -1177,9 +1559,7 @@
         ),
         name="backward_part",
     )(
-        labels_down,
-        labels_across,
-        normed,
+        labels,
         query_feature,
         key_feature,
         values,
@@ -1187,35 +1567,57 @@
         denominator,
         key_sum,
         hidden_low,
-        hidden_share,
-        gradient_share,
-        pixel_share,
         gain_part,
         prefix_low,
         latest,
-        middle,
-        down_weight,
         query_weight,
         key_weight,
         value_weight,
         out_weight,
         first_gain.reshape(1, model),
+        near_two,
+        normed,
+        hidden_share,
+        gradient_share,
+        pixel_share,
         wide_gradient,
     )
-    start = lax.axis_index("rows") * s.cut
-    second_part, first_part = (lax.dynamic_slice(gains[i], (start,), (s.cut,)) for i in range(2))
-    narrow = [narrow_out[:, i * s.width : (i + 1) * s.width] for i in range(4)]
+    outs = [
+        shape((s.cut, s.units), WIDE),
+        shape((s.units, s.cut), WIDE),
+        shape((s.width, s.cut), WIDE),
+        *[shape((s.cut, s.width), WIDE)] * 3,
+        *[shape((1, s.cut), WIDE)] * 2,
+        shape(whole, WIDE),
+        shape((tokens, model), LOW),
+    ]
+    up_part, down_part, out_part, query_part, key_part, value_part, first_part, second_part, pixel_part, result = (
+        pl.pallas_call(
+            functools.partial(finish_kernel, s),
+            out_shape=outs,
+            in_specs=vmem(4) + [any_space] * 2,
+            out_specs=vmem(8) + [any_space] * 2,
+            scratch_shapes=[
+                pltpu.VMEM(whole, WIDE),
+                pltpu.VMEM((tokens, model), LOW),
+                dma(2, s.chunks),
+                dma(2, s.chunks),
+            ],
+            compiler_params=pltpu.CompilerParams(vmem_limit_bytes=60 << 20),
+            name="finish_part",
+        )(first_out, wide_out, narrow_out, gains, pixel_wide, result_low)
+    )
     return (
         result,
-        pixel_gradient.reshape(tokens, model),
-        first_part,
-        narrow[1],
-        narrow[2],
-        narrow[3],
-        narrow[0].T,
-        second_part,
-        up_out,
-        down_out.T,
+        pixel_part.reshape(tokens, model),
+        first_part.reshape(s.cut),
+        query_part,
+        key_part,
+        value_part,
+        out_part,
+        second_part.reshape(s.cut),
+        up_part,
+        down_part,
     )
 
 

time: 304 us -> 238 us (0.78)
  Pallas kernels: 289 us -> 237 us
  local copies, waits for them, and re-layouts: 12.9 us -> 0 us
    pallas_call x1, Pallas kernels: 180 us -> 132 us  [on_device(): pl.pallas_call(functools.partial(backward_kernel, s), out_shape=outs, in_...]
    pallas_call x1, Pallas kernels: 109 us -> 97.2 us  [on_device(): pl.pallas_call(functools.partial(forward_kernel, s), out_shape=outs, in_s...]
    unnamed x13 -> x0, local copies, waits for them, and re-layouts: 8.55 us -> none
    pallas_call x0 -> x1, Pallas kernels: none -> 7.8 us  [on_device(): pl.pallas_call(functools.partial(finish_kernel, s), out_shape=outs, in_sp...]
where the time goes in v3:
time: 238 us
  Pallas kernels  237 us (100%)
    pallas_call x1, Pallas kernels, on_device(): pl.pallas_call(functools.partial(backward_kernel, s), out_shape=outs, in_...  132 us
    pallas_call x1, Pallas kernels, on_device(): pl.pallas_call(functools.partial(forward_kernel, s), out_shape=outs, in_s...  97.2 us
    pallas_call x1, Pallas kernels, on_device(): pl.pallas_call(functools.partial(finish_kernel, s), out_shape=outs, in_sp...  7.8 us

profile of v3, /device:TPU:0, one launch (start us, length us, event | category | flops | bytes accessed | tf_op | source)
XLA Modules:
  0.0 237.8 jit_solution(1061995693421735034)
XLA Ops:
  0.6 97.2 %forward_part.1 = (bf16[1024,1024]{1,0:T(8,128)(2,1)}, f32[4,64,1024]{2,1,0:T(8,128)}, f32[4,64,1024]{2,1,0:T(8,128)}, bf16[4,64,1024]{2,1,0:T(8,128)(2,1)}, f32...) custom-call(bf16[4,2,2,64,1024]{4,3,2,1,0:T(8,128)(2,1)} %bitcast.8,, ...), custom_call_target="tpu_custom_call" | custom-call | tf_op jit(solution)/shard_map/forward_part/pallas_call | solution.py:1428
  97.9 132.0 %backward_part.1 = (f32[8,1024]{1,0:T(8,128)}, f32[128,1536]{1,0:T(8,128)}, f32[128,1024]{1,0:T(8,128)}, f32[4,2,2,64,1024]{4,3,2,1,0:T(8,128)}, bf16[1024,1024]{1,0:T(8,128)(2,1)}) custom-call(s32[4,1,256]{2,1,0:T(1,128)} %bitcast.11, bf16[1024,256]{1,0:T(8,128)(2,1)} %get-tuple-element.43.query_feature, bf16[1024,256]{1,0:T(8,128)(2,1)} %get-tuple-element.44.key_feature, ...), custom_call_target="tpu_custom_call" | custom-call | tf_op jit(solution)/shard_map/backward_part/pallas_call | solution.py:1497
  229.9 7.8 %finish_part.1 = (f32[128,1024]{1,0:T(8,128)}, f32[1024,128]{1,0:T(8,128)}, f32[256,128]{1,0:T(8,128)}, f32[128,256]{1,0:T(8,128)}, f32[128,256]{1,0:T(8,128)}, ...) custom-call(f32[128,512]{1,0:T(8,128)} %get-tuple-element.42.first_o, ...), custom_call_target="tpu_custom_call" | custom-call | tf_op jit(solution)/shard_map/finish_part/pallas_call | solution.py:1595

commit v4 on v3

--- a/solution.py
+++ b/solution.py
@@ -15,8 +15,8 @@
 WIDE = jnp.float32
 LANES = 128
 TILE = 256
-AHEAD = 2
-FIRST = 4
+AHEAD = 3
+FIRST = 6
 
 
 def dot(left, right):
@@ -303,14 +303,14 @@
     def at(self, m):
         return m >> self.first_bit
 
-    def pair_copy(self, m):
+    def pair_copy(self, m, x):
         send, receive = self.pair_sems
-        return remote(
-            self.source(self.piece(m)), self.pairs.at[m >> 1], send.at[m >> 1], receive.at[m >> 1], self.to_z(0)
-        )
+        at = (m >> 1, x)
+        return remote(self.source(self.piece(m)).at[x], self.pairs.at[at], send.at[at], receive.at[at], self.to_z(0))
 
     def join_pair(self, m, own):
-        self.pair_copy(m + 1).wait_recv()
+        for x in range(self.p.s.nx):
+            self.pair_copy(m + 1, x).wait_recv()
         self.pairs[m >> 1] = self.pairs[m >> 1] + own
 
     def near_copy(self, m, step):
@@ -354,7 +354,8 @@
     def sent(self):
         if self.pairs is not None:
             for m in self.odd:
-                self.pair_copy(m).wait_send()
+                for x in range(self.p.s.nx):
+                    self.pair_copy(m, x).wait_send()
         for m in self.order:
             for step in range(1, self.p.s.nx):
                 self.near_copy(m, step).wait_send()
@@ -794,6 +795,7 @@
         second_norm_back(k)
         first_join(k - end + 2)
         rest_outer(k - end + 3)
+    first.settle(order[1])
     for turn in range(3, s.nz):
         rest_outer(turn)
 
@@ -806,18 +808,19 @@
             parts[k, :, :, :, cols] = dot(low, down_weight[:, cols]).reshape(shares)
         two.start(k)
 
-    for turn in range(2, s.nz):
+    for turn in range(2, s.nz - 1):
         first_join(turn)
-        if order[turn] % 2:
-            first.settle(order[turn] + 1)
+        if order[turn] % 2 == 0:
+            first.settle(order[turn])
+    for k in range(end - 2):
+        hidden_gather.forward(k)
     for k in range(s.chunks):
         two.join(k)
         pixel_share[k] = pixels[k, p.c, p.y]
-    for k in range(end - 2):
-        hidden_gather.forward(k)
+    first_join(s.nz - 1)
+    hidden_gather.forward(end - 2)
     first.settle(0)
-    for k in range(end - 2, end):
-        hidden_gather.forward(k)
+    hidden_gather.forward(end - 1)
 
     for k in range(s.chunks):
         hidden_gather.finish(k)
@@ -839,6 +842,32 @@
 def backward_kernel(
     s,
     crop_ids,
+    gain_part,
+    prefix_low,
+    latest,
+    first_gain,
+    near_two,
+    normed_source,
+    hidden_source,
+    gradient_source,
+    pixel_source,
+    wide_gradient,
+    query_feature_source,
+    key_feature_source,
+    values_source,
+    attended_source,
+    denominator_source,
+    key_sum_source,
+    hidden_low_source,
+    query_weight_source,
+    key_weight_source,
+    value_weight_source,
+    out_weight_source,
+    gains,
+    wide_out,
+    narrow_out,
+    pixel_out,
+    result_out,
     query_feature,
     key_feature,
     values,
@@ -846,25 +875,10 @@
     denominator,
     key_sum,
     hidden_low,
-    gain_part,
-    prefix_low,
-    latest,
     query_weight,
     key_weight,
     value_weight,
     out_weight,
-    first_gain,
-    near_two,
-    normed_source,
-    hidden_source,
-    gradient_source,
-    pixel_source,
-    wide_gradient,
-    gains,
-    wide_out,
-    narrow_out,
-    pixel_out,
-    result_out,
     normed,
     hidden_share,
     gradient_share,
@@ -905,6 +919,7 @@
     gain_x,
     gain_z,
     load_sem,
+    input_sem,
     message_send,
     message_recv,
     two_far_send,
@@ -939,6 +954,26 @@
     pixel_sem,
 ):
     p = Place(s)
+    inputs = [
+        pltpu.make_async_copy(source, target, input_sem.at[i])
+        for i, (source, target) in enumerate(
+            (
+                (hidden_low_source, hidden_low),
+                (out_weight_source, out_weight),
+                (denominator_source, denominator),
+                (attended_source, attended),
+                (query_feature_source, query_feature),
+                (key_feature_source, key_feature),
+                (values_source, values),
+                (key_sum_source, key_sum),
+                (query_weight_source, query_weight),
+                (key_weight_source, key_weight),
+                (value_weight_source, value_weight),
+            )
+        )
+    ]
+    for load in inputs:
+        load.start()
     p.meet()
     two = Reduce(p, None, near_two, far_two, (None, None, two_far_send, two_far_recv))
     four = Reduce(p, parts, near_four, far_four, (four_near_send, four_near_recv, four_far_send, four_far_recv))
@@ -968,9 +1003,23 @@
 
     narrow = (narrow_job(0), narrow_job(1))
     jobs = (wide, split) + narrow
-    steps = [(job, m) for job in jobs for m in job.order]
-    flight = {"next": 0, "ready": s.nz, "taken": 0}
+    whole_wide = [(wide, m) for m in wide.order]
+    whole_split = [(split, m) for m in split.order]
+    whole_narrow = [(job, m) for job in narrow for m in job.order]
+    steps = whole_wide + whole_split[:1] + whole_narrow[:1] + whole_split[1:] + whole_narrow[1:]
+    flight = {"next": 0, "taken": 0}
+    ready = list(whole_wide)
     pending = []
+
+    def push(limit):
+        while flight["next"] <= min(limit, len(steps) - 1) and steps[flight["next"]] in ready:
+            job, m = steps[flight["next"]]
+            job.start(m)
+            flight["next"] += 1
+
+    def admit(entries):
+        ready.extend(entries)
+        push(flight["taken"] + AHEAD - 1)
 
     def settle_ready(at):
         for entry in list(pending):
@@ -978,12 +1027,6 @@
                 entry[1].settle(entry[2])
                 pending.remove(entry)
 
-    def push(limit):
-        while flight["next"] <= limit and flight["next"] < flight["ready"]:
-            job, m = steps[flight["next"]]
-            job.start(m)
-            flight["next"] += 1
-
     def own_load(turn):
         source = wide_gradient.at[wide.piece(wide.order[turn]), p.x, :, s.split :]
         return pltpu.make_async_copy(source, own_wide.at[turn % 2], own_sem.at[turn % 2])
@@ -994,8 +1037,9 @@
 
     def take():
         at = flight["taken"]
+        assert flight["next"] > at
+        job, m = steps[at]
         flight["taken"] = at + 1
-        job, m = steps[at]
         if job is wide:
             own_load(at).wait()
             wide.join(m, own_wide[at % 2])
@@ -1009,11 +1053,15 @@
         if (m >> job.first_bit) & 1:
             job.settle(m)
         else:
-            pending.append((at + 1 if m else at + 2, job, m))
+            pending.append((at + 2 if m else at + 4, job, m))
         settle_ready(at)
 
-    for m in split.odd:
-        split.pair_copy(m).start()
+    def take_while(*names):
+        while flight["taken"] < len(steps) and steps[flight["taken"]][0] in names:
+            take()
+
+    pair_copies = [(m, x) for m in split.odd for x in range(s.nx)]
+    split.pair_copy(*pair_copies[0]).start()
     push(0)
     for k in range(s.chunks):
         two.spread(k)
@@ -1044,6 +1092,9 @@
     total[...] = jnp.zeros_like(total)
     ones[...] = block_ones(s.width)
 
+    for load in inputs:
+        load.wait()
+
     @pl.loop(0, s.chunks)
     def _(k):
         at = chunk_rows(s, k)
@@ -1062,7 +1113,9 @@
 
     write_message(s, messages.at[0], state, total[0:1, :], first)
     send_messages(p, messages, message_send, message_recv)
-    push(AHEAD - 1)
+    for entry in pair_copies[1 : s.nx]:
+        split.pair_copy(*entry).start()
+    push(1)
 
     @pl.loop(0, s.chunks)
     def _(i):
@@ -1083,6 +1136,8 @@
         lax.fori_loop(0, i + 1, over, 0)
 
     take()
+    for entry in pair_copies[s.nx :]:
+        split.pair_copy(*entry).start()
 
     @pl.loop(0, s.chunks)
     def _(j):
@@ -1109,7 +1164,6 @@
 
     for load in loads:
         load.wait()
-    take()
 
     @pl.loop(0, s.chunks)
     def _(k):
@@ -1120,6 +1174,7 @@
         def _():
             result_gather.start(k)
 
+    take()
     take_messages(p, messages, message_send, message_recv)
     suffix_total, following = join_messages(p, messages, suffix_low, s.rows - 1, p.row < s.rows - 1, False)
 
@@ -1152,12 +1207,16 @@
     def _(k):
         four.middle(k)
 
+    for k in range(s.chunks // 2, s.chunks):
+        result_gather.start(k)
     take()
-    for m in split.order:
+
+    def split_ready(m):
         pairs_load(m).wait()
         split.join_pair(m, own_pairs[m >> 1])
-    flight["ready"] = len(wide.order) + len(split.order)
-
+        admit([(split, m)])
+
+    split_ready(split.order[0])
     span = s.nx * s.cut
     for piece in range(s.nz):
         cols = slice(piece * span, (piece + 1) * span)
@@ -1167,15 +1226,15 @@
         for part in range(3):
             product = dot_left(normed[:, cols], narrow_low[part])
             narrow_gradient[piece, :, :, (part + 1) * s.width : (part + 2) * s.width] = product.reshape(shape)
-    flight["ready"] = len(steps)
+    admit(whole_narrow)
+    take_while(wide)
+    for m in split.order[1:]:
+        split_ready(m)
+    gain_x[0] = gain_part[...]
 
     def take_until_left(count):
         while len(steps) - flight["taken"] > count:
             take()
-
-    left = 2 * s.nz
-    take_until_left(left + len(split.order))
-    gain_x[0] = gain_part[...]
 
     def result_copy(k):
         rows = pl.ds(k * s.chunk, s.chunk)
@@ -1191,11 +1250,13 @@
         pixel_gradient[k, p.c, p.y] = gradient_share[k] + normalise_back(unit, scale, first_gain[...], grad)
         pixel_gather.start(k)
 
-    for k in range(s.chunks // 2):
+    first_norm_back(0)
+    take()
+    for k in range(1, s.chunks - 1):
         first_norm_back(k)
-    take_until_left(left + len(split.order) // 2)
-    for k in range(s.chunks // 2, s.chunks):
-        first_norm_back(k)
+        take_while(split)
+    take_until_left(2 * s.nz - 1)
+    first_norm_back(s.chunks - 1)
 
     def gain_copies(index, buffer, device):
         return [
@@ -1221,23 +1282,20 @@
         (2, gain_heads, p.along_heads),
     )
     gain_start(*rounds[0])
-    for k in range(s.chunks // 2, s.chunks):
-        result_gather.start(k)
-    take_until_left(left)
     for k in range(s.chunks // 2):
         result_gather.forward(k)
-    take_until_left(left - 2)
+    take_until_left(2 * s.nz - 3)
+    for k in range(s.chunks // 2, s.chunks):
+        result_gather.forward(k)
     gain_z[0] = gain_total(*rounds[0])
     gain_start(*rounds[1])
     for k in range(s.chunks // 2):
         pixel_gather.forward(k)
-    take_until_left(left - 4)
+    take_until_left(3)
     gain_heads[0] = gain_total(*rounds[1])
     gain_start(*rounds[2])
     for k in range(s.chunks // 2, s.chunks):
         pixel_gather.forward(k)
-    for k in range(s.chunks // 2, s.chunks):
-        result_gather.forward(k)
     take_until_left(2)
     for k in range(s.chunks):
         pixel_gather.finish(k)
@@ -1248,9 +1306,9 @@
         result_copy(k).start()
     gains[...] = gain_total(*rounds[2])
     take_until_left(0)
+    settle_ready(len(steps) + 4)
     wide_out[:, s.split :] = wide.total()
     wide_out[:, 0 : s.split] = split.total()
-    settle_ready(len(steps) + 2)
     for job, side in zip(narrow, sides):
         narrow_out[:, side] = job.total()
     for k in range(s.chunks):
@@ -1267,28 +1325,35 @@
 
 def finish_kernel(
     s,
-    first_out,
-    wide_out,
-    narrow_out,
     gains,
+    first_source,
+    wide_source,
+    narrow_source,
     pixel_source,
     result_source,
+    first_gain,
+    second_gain,
     up_gradient,
     down_gradient,
     out_gradient,
     query_gradient,
     key_gradient,
     value_gradient,
-    first_gain,
-    second_gain,
     pixel_gradient,
     result,
     pixel_rows,
     result_rows,
+    first_out,
+    wide_out,
+    narrow_out,
+    down_turned,
+    out_turned,
     read_sem,
     write_sem,
+    small_sem,
 ):
     row = lax.axis_index("rows")
+    rest = s.units - s.first
 
     def places(i, k):
         rows = pl.ds(k * s.chunk, s.chunk)
@@ -1304,26 +1369,46 @@
         unused, between, target = places(i, k)
         return pltpu.make_async_copy(between, target, write_sem.at[i, k])
 
+    def small(at, source, target):
+        return pltpu.make_async_copy(source, target, small_sem.at[at])
+
+    reads = [
+        small(0, wide_source, wide_out),
+        small(1, narrow_source, narrow_out),
+        small(2, first_source, first_out),
+    ]
     moves = [(i, k) for k in range(s.chunks) for i in range(2)]
+    for copy in reads:
+        copy.start()
     for move in moves:
         read(*move).start()
-    rest = s.units - s.first
-    up_gradient[:, 0 : s.first] = first_out[...]
-    up_gradient[:, s.first :] = wide_out[:, 0:rest]
-    down_gradient[...] = wide_out[:, rest:].T
-    out_gradient[...] = narrow_out[:, 0 : s.width].T
-    for i, target in enumerate((query_gradient, key_gradient, value_gradient)):
-        target[...] = narrow_out[:, (i + 1) * s.width : (i + 2) * s.width]
     own = jnp.zeros((8, s.cut), WIDE)
     for at in range(s.rows):
         own = own + jnp.where(row == at, gains[:, at * s.cut : (at + 1) * s.cut], 0.0)
     second_gain[...] = own[0:1]
     first_gain[...] = own[1:2]
+    for copy in reads:
+        copy.wait()
+    writes = [
+        small(3, first_out, up_gradient.at[:, 0 : s.first]),
+        small(4, wide_out.at[:, 0:rest], up_gradient.at[:, s.first :]),
+    ]
+    for i, target in enumerate((query_gradient, key_gradient, value_gradient)):
+        writes.append(small(5 + i, narrow_out.at[:, (i + 1) * s.width : (i + 2) * s.width], target))
+    for copy in writes:
+        copy.start()
+    down_turned[...] = wide_out[:, rest:].T
+    out_turned[...] = narrow_out[:, 0 : s.width].T
+    for at, source, target in ((8, down_turned, down_gradient), (9, out_turned, out_gradient)):
+        writes.append(small(at, source, target))
+        writes[-1].start()
     for move in moves:
         read(*move).wait()
         write(*move).start()
     for move in moves:
         write(*move).wait()
+    for copy in writes:
+        copy.wait()
 
 
 def vmem(count):
@@ -1497,9 +1582,14 @@
     gains, wide_out, narrow_out, pixel_wide, result_low = pl.pallas_call(
         functools.partial(backward_kernel, s),
         out_shape=outs,
-        in_specs=vmem(16) + [any_space] * 6,
+        in_specs=vmem(5) + [any_space] * 17,
         out_specs=vmem(3) + [any_space] * 2,
         scratch_shapes=[
+            *[pltpu.VMEM(size, LOW) for size in lows[1:]],
+            *[pltpu.VMEM(size, WIDE) for size in wides],
+            pltpu.VMEM((tokens, model), LOW),
+            *[pltpu.VMEM((model, s.width), LOW)] * 3,
+            pltpu.VMEM((s.width, model), LOW),
             pltpu.VMEM((tokens, model), LOW),
             pltpu.VMEM(share, WIDE),
             pltpu.VMEM(share, WIDE),
@@ -1535,6 +1625,7 @@
             pltpu.VMEM((s.nx, 8, model), WIDE),
             pltpu.VMEM((s.nz, 8, model), WIDE),
             dma(5),
+            dma(11),
             dma(rows),
             dma(rows),
             *reduce_sems()[2:],
@@ -1543,8 +1634,8 @@
             *gather_sems(),
             *scatter_sems(),
             *scatter_sems(),
-            dma(half),
-            dma(half),
+            dma(half, s.nx),
+            dma(half, s.nx),
             *[dma(2, s.nx - 1, s.nz)] * 2,
             *[dma(2, s.nz - 1)] * 2,
             dma(3, max(heads, s.nx, s.nz)),
@@ -1560,6 +1651,16 @@
         name="backward_part",
     )(
         labels,
+        gain_part,
+        prefix_low,
+        latest,
+        first_gain.reshape(1, model),
+        near_two,
+        normed,
+        hidden_share,
+        gradient_share,
+        pixel_share,
+        wide_gradient,
         query_feature,
         key_feature,
         values,
@@ -1567,45 +1668,41 @@
         denominator,
         key_sum,
         hidden_low,
-        gain_part,
-        prefix_low,
-        latest,
         query_weight,
         key_weight,
         value_weight,
         out_weight,
-        first_gain.reshape(1, model),
-        near_two,
-        normed,
-        hidden_share,
-        gradient_share,
-        pixel_share,
-        wide_gradient,
     )
     outs = [
+        *[shape((1, s.cut), WIDE)] * 2,
         shape((s.cut, s.units), WIDE),
         shape((s.units, s.cut), WIDE),
         shape((s.width, s.cut), WIDE),
         *[shape((s.cut, s.width), WIDE)] * 3,
-        *[shape((1, s.cut), WIDE)] * 2,
         shape(whole, WIDE),
         shape((tokens, model), LOW),
     ]
-    up_part, down_part, out_part, query_part, key_part, value_part, first_part, second_part, pixel_part, result = (
+    first_part, second_part, up_part, down_part, out_part, query_part, key_part, value_part, pixel_part, result = (
         pl.pallas_call(
             functools.partial(finish_kernel, s),
             out_shape=outs,
-            in_specs=vmem(4) + [any_space] * 2,
-            out_specs=vmem(8) + [any_space] * 2,
+            in_specs=vmem(1) + [any_space] * 5,
+            out_specs=vmem(2) + [any_space] * 8,
             scratch_shapes=[
                 pltpu.VMEM(whole, WIDE),
                 pltpu.VMEM((tokens, model), LOW),
+                pltpu.VMEM((s.cut, s.first), WIDE),
+                pltpu.VMEM((s.cut, s.wide), WIDE),
+                pltpu.VMEM((s.cut, s.narrow), WIDE),
+                pltpu.VMEM((s.units, s.cut), WIDE),
+                pltpu.VMEM((s.width, s.cut), WIDE),
                 dma(2, s.chunks),
                 dma(2, s.chunks),
+                dma(10),
             ],
             compiler_params=pltpu.CompilerParams(vmem_limit_bytes=60 << 20),
             name="finish_part",
-        )(first_out, wide_out, narrow_out, gains, pixel_wide, result_low)
+        )(gains, first_out, wide_out, narrow_out, pixel_wide, result_low)
     )
     return (
         result,

time: 238 us -> 233 us (0.979)
  Pallas kernels: 237 us -> 232 us
    pallas_call x1, Pallas kernels: 132 us -> 119 us  [on_device(): pl.pallas_call(functools.partial(backward_kernel, s), out_shape=outs, in_...]
    pallas_call x1, Pallas kernels: 97.2 us -> 105 us  [on_device(): pl.pallas_call(functools.partial(forward_kernel, s), out_shape=outs, in_s...]
where the time goes in v4:
time: 233 us
  Pallas kernels  232 us (100%)
    pallas_call x1, Pallas kernels, on_device(): pl.pallas_call(functools.partial(backward_kernel, s), out_shape=outs, in_...  119 us
    pallas_call x1, Pallas kernels, on_device(): pl.pallas_call(functools.partial(forward_kernel, s), out_shape=outs, in_s...  105 us
    pallas_call x1, Pallas kernels, on_device(): pl.pallas_call(functools.partial(finish_kernel, s), out_shape=outs, in_sp...  7.71 us

profile of v4, /device:TPU:0, one launch (start us, length us, event | category | flops | bytes accessed | tf_op | source)
XLA Modules:
  0.0 232.7 jit_solution(11073889294829148856)
XLA Ops:
  0.6 104.8 %forward_part.1 = (bf16[1024,1024]{1,0:T(8,128)(2,1)}, f32[4,64,1024]{2,1,0:T(8,128)}, f32[4,64,1024]{2,1,0:T(8,128)}, bf16[4,64,1024]{2,1,0:T(8,128)(2,1)}, f32...) custom-call(bf16[4,2,2,64,1024]{4,3,2,1,0:T(8,128)(2,1)} %bitcast.8,, ...), custom_call_target="tpu_custom_call" | custom-call | tf_op jit(solution)/shard_map/forward_part/pallas_call | solution.py:1513
  105.5 119.4 %backward_part.1 = (f32[8,1024]{1,0:T(8,128)}, f32[128,1280]{1,0:T(8,128)}, f32[128,1024]{1,0:T(8,128)}, f32[4,2,2,64,1024]{4,3,2,1,0:T(8,128)}, bf16[1024,1024]{1,0:T(8,128)(2,1)}) custom-call(s32[4,1,256]{2,1,0:T(1,128)} %bitcast.11, f32[8,1024]{1,0:T(8,128)} %get-tuple-element.42.gain_part, bf16[256,256]{1,0:T(8,128)(2,1)} %get-tuple-element.43.prefix_low, ...), custom_call_target="tpu_custom_call" | custom-call | tf_op jit(solution)/shard_map/backward_part/pallas_call | solution.py:1582
  224.9 7.7 %finish_part.1 = (f32[1,128]{1,0:T(1,128)}, f32[1,128]{1,0:T(1,128)}, f32[128,1024]{1,0:T(8,128)}, f32[1024,128]{1,0:T(8,128)}, f32[256,128]{1,0:T(8,128)}, /*in...) custom-call(f32[8,1024]{1,0:T(8,128)} %get-tuple-element.58.gains, ...), custom_call_target="tpu_custom_call" | custom-call | tf_op jit(solution)/shard_map/finish_part/pallas_call | solution.py:1686

commit v5 on v4

--- a/solution.py
+++ b/solution.py
@@ -15,7 +15,7 @@
 WIDE = jnp.float32
 LANES = 128
 TILE = 256
-AHEAD = 3
+AHEAD = 2
 FIRST = 6
 
 

time: 233 us -> 232 us (level)
  no operation moved by 1% of the time
where the time goes in v5:
time: 232 us
  Pallas kernels  231 us (100%)
    pallas_call x1, Pallas kernels, on_device(): pl.pallas_call(functools.partial(backward_kernel, s), out_shape=outs, in_...  118 us
    pallas_call x1, Pallas kernels, on_device(): pl.pallas_call(functools.partial(forward_kernel, s), out_shape=outs, in_s...  105 us
    pallas_call x1, Pallas kernels, on_device(): pl.pallas_call(functools.partial(finish_kernel, s), out_shape=outs, in_sp...  7.71 us

profile of v5, /device:TPU:0, one launch (start us, length us, event | category | flops | bytes accessed | tf_op | source)
XLA Modules:
  0.0 231.8 jit_solution(15312637648704850381)
XLA Ops:
  0.6 104.8 %forward_part.1 = (bf16[1024,1024]{1,0:T(8,128)(2,1)}, f32[4,64,1024]{2,1,0:T(8,128)}, f32[4,64,1024]{2,1,0:T(8,128)}, bf16[4,64,1024]{2,1,0:T(8,128)(2,1)}, f32...) custom-call(bf16[4,2,2,64,1024]{4,3,2,1,0:T(8,128)(2,1)} %bitcast.8,, ...), custom_call_target="tpu_custom_call" | custom-call | tf_op jit(solution)/shard_map/forward_part/pallas_call | solution.py:1513
  105.5 118.4 %backward_part.1 = (f32[8,1024]{1,0:T(8,128)}, f32[128,1280]{1,0:T(8,128)}, f32[128,1024]{1,0:T(8,128)}, f32[4,2,2,64,1024]{4,3,2,1,0:T(8,128)}, bf16[1024,1024]{1,0:T(8,128)(2,1)}) custom-call(s32[4,1,256]{2,1,0:T(1,128)} %bitcast.11, f32[8,1024]{1,0:T(8,128)} %get-tuple-element.42.gain_part, bf16[256,256]{1,0:T(8,128)(2,1)} %get-tuple-element.43.prefix_low, ...), custom_call_target="tpu_custom_call" | custom-call | tf_op jit(solution)/shard_map/backward_part/pallas_call | solution.py:1582
  223.9 7.7 %finish_part.1 = (f32[1,128]{1,0:T(1,128)}, f32[1,128]{1,0:T(1,128)}, f32[128,1024]{1,0:T(8,128)}, f32[1024,128]{1,0:T(8,128)}, f32[256,128]{1,0:T(8,128)}, /*in...) custom-call(f32[8,1024]{1,0:T(8,128)} %get-tuple-element.58.gains, ...), custom_call_target="tpu_custom_call" | custom-call | tf_op jit(solution)/shard_map/finish_part/pallas_call | solution.py:1686
